TPU v7x, 32 devices: a whole 2x2x4 slice. The times are simulated.
32 devices in a mesh: sec: 8 (over z, core), bond: 4 (over y, x).
Axes of the slice: x: 2, y: 2, z: 4, core: 2. Of those that a mesh axis runs over, the one named last changes fastest.
Arguments:
- left_env: bfloat16 [8, 512, 8, 512], P('sec', 'bond'), may hold values from -6 to 6
- site: bfloat16 [8, 512, 4, 512], P('sec', 'bond'), may hold values from -0.125 to 0.125
- psi: bfloat16 [8, 512, 4, 4, 512], P('sec', 'bond'), may hold values from -0.25 to 0.25
- right_env: bfloat16 [8, 8, 512, 512], P('sec'), may hold values from -0.09375 to 0.09375
- mpo: bfloat16 [8, 8, 4, 4], replicated, may hold values from -1 to 1
Outputs:
- new_left: bfloat16 [8, 512, 8, 512], P('sec', 'bond')
- product: bfloat16 [8, 512, 4, 4, 512], P('sec', 'bond')
All inputs are finite; a program needn't handle non-finite values.
Results may differ from a plain program's by a relative error of at most 0.0095.
Values may be sent and summed in bfloat16 or wider, within the bound.
A program may use at most 128 MiB of HBM per device.

v0:
```python
import functools

import jax
import jax.numpy as jnp
from jax import lax
from jax.experimental import pallas as pl
from jax.experimental.pallas import tpu as pltpu
from jax.sharding import PartitionSpec as P

MESH = pl.DeviceIdType.MESH
BF16 = jnp.bfloat16
F32 = jnp.float32


def mm(a, b):
    return jnp.dot(a, b, preferred_element_type=F32)


def kernel(
    dims,
    left_h, site_h, psi_h, right_h, mpo_h,
    new_left, product,
    left, site_raw, psi_raw, mpo, right,
    site_own, psi_own, site, site_tr, mix, pair,
    second, part, rs1, send2, rs2, nl_own, nl_in, psi, mixed, proj, acc,
    local_sem, send_sem, recv_sem,
):
    rows, width, phys, chi, group, cuts, batch = dims
    n_bond = 4
    pq = phys * phys
    sec = lax.axis_index("sec")
    me = lax.axis_index("bond")
    n_sec = lax.axis_size("sec")
    next_sec = lax.rem(sec + 1, n_sec)
    prev_sec = lax.rem(sec + n_sec - 1, n_sec)
    bx = (me // 2) * 2 + 1 - lax.rem(me, 2)
    by = lax.rem(me + 2, n_bond)
    bd = lax.rem(bx + 2, n_bond)
    to_x = {"bond": bx}
    to_y = {"bond": by}
    to_next = {"sec": next_sec}

    def block(owner):
        return pl.ds(pl.multiple_of(owner * rows, rows), rows)

    loads = {}
    for i, (name, src, dst) in enumerate((
        ("site", site_h, site_raw),
        ("psi", psi_h, psi_raw),
        ("mpo", mpo_h, mpo),
        ("left", left_h, left),
        ("right", right_h, right),
    )):
        loads[name] = pltpu.make_async_copy(src, dst, local_sem.at[i])
        loads[name].start()

    barrier = pltpu.get_barrier_semaphore()
    for target in (to_x, to_y, to_next, {"sec": prev_sec}):
        pl.semaphore_signal(barrier, inc=1, device_id=target, device_id_type=MESH)
    pl.semaphore_wait(barrier, 4)

    started = []
    counter = {}

    def slot(key):
        return counter.setdefault(key, len(counter))

    def send(key, src, dst, target):
        i = slot(key)
        copy = pltpu.make_async_remote_copy(
            src_ref=src, dst_ref=dst, send_sem=send_sem.at[i], recv_sem=recv_sem.at[i],
            device_id=target, device_id_type=MESH,
        )
        copy.start()
        started.append(copy)

    def arrive(key, dst, target):
        i = slot(key)
        pltpu.make_async_remote_copy(
            src_ref=dst, dst_ref=dst, send_sem=send_sem.at[i], recv_sem=recv_sem.at[i],
            device_id=target, device_id_type=MESH,
        ).wait_recv()

    lanes = chi // cuts

    loads["site"].wait()
    flat = site_raw[...].astype(F32).reshape(rows * phys, chi)
    for i in range(cuts):
        acc[i, :rows * phys, :] = flat[:, i * lanes:(i + 1) * lanes]
    for t in range(phys):
        for i in range(cuts):
            tile = acc[i, pl.ds(t, rows, stride=phys), :]
            site_own[t, :, i * lanes:(i + 1) * lanes] = tile.astype(BF16)
            site_tr[i * lanes:(i + 1) * lanes, t * rows:(t + 1) * rows] = tile.T.astype(BF16)
    site_here = pltpu.make_async_copy(site_own, site.at[:, block(me), :], local_sem.at[5])
    site_here.start()
    send("site_x", site_own, site.at[:, block(me), :], to_x)
    send("site_y", site_own, site.at[:, block(me), :], to_y)

    loads["psi"].wait()
    tall = 8

    @pl.loop(0, rows // tall)
    def _(g):
        flat = psi_raw[pl.ds(pl.multiple_of(g * tall, tall), tall)].astype(F32)
        flat = flat.reshape(tall * pq, chi)
        where = pl.ds(pl.multiple_of(g * tall * pq, tall * pq), tall * pq)
        for i in range(cuts):
            acc[i, where, :] = flat[:, i * lanes:(i + 1) * lanes]

    half = pq // 4

    def region(q, owner, sub=None):
        if sub is None:
            return psi.at[q, :, block(owner), :]
        return psi.at[q, pl.ds(sub * half, half), block(owner), :]

    for q in range(cuts):
        for t in range(pq):
            at = (t % 2) * lanes
            tile = acc[q, pl.ds(t, rows, stride=pq), :]
            psi_own[q, t // 2, :, at:at + lanes] = tile.astype(BF16)
        if q > 0:
            send(("shift", q - 1), psi_own.at[q - 1], region(q - 1, me), to_next)
    send(("shift", cuts - 1), psi_own.at[cuts - 1], region(cuts - 1, me), to_next)

    def spread(q):
        arrive(("shift", q), region(q, me), to_next)
        send(("psi_x", q), region(q, me), region(q, me), to_x)
        send(("psi_y", q), region(q, me), region(q, me), to_y)

    def relay(q):
        arrive(("psi_x", q), region(q, bx), to_x)
        send(("psi_xy", q), region(q, bx, 0), region(q, bx, 0), to_y)
        arrive(("psi_y", q), region(q, by), to_y)
        send(("psi_yx", q), region(q, by, 1), region(q, by, 1), to_x)

    def complete(q):
        arrive(("psi_xy", q), region(q, bd, 0), to_y)
        arrive(("psi_yx", q), region(q, bd, 1), to_x)

    loads["mpo"].wait()

    def iota(shape, axis):
        return lax.broadcasted_iota(jnp.int32, shape, axis)

    def one_hot(condition):
        return jnp.where(condition, 1.0, 0.0).astype(BF16)

    small = phys * width
    big = small * group
    tall_code = lax.div(iota((big, small), 0), group)
    spread_rows = one_hot(tall_code == iota((big, small), 1))
    col = iota((small, big), 1)
    col_code = lax.div(col, group * width) * width + lax.rem(col, width)
    spread_cols = one_hot(col_code == iota((small, big), 0))
    wide = mm(mm(spread_rows, mpo[...]).astype(BF16), spread_cols)
    same = lax.rem(iota((big, big), 0), group) == lax.rem(lax.div(iota((big, big), 1), width), group)
    mix[...] = jnp.where(same, wide, 0.0).astype(BF16)

    side = width * pq
    col = iota((small, side), 1)
    col_m = lax.rem(col, width)
    col_sv = lax.rem(lax.div(col, width), pq // 2) * 2 + lax.div(col, width * (pq // 2))
    col_s, col_v = lax.div(col_sv, phys), lax.rem(col_sv, phys)
    row = iota((side, small), 0)
    row_k, row_u, row_w = lax.div(row, pq), lax.rem(lax.div(row, phys), phys), lax.rem(row, phys)
    code_c, code_r = iota((small, side), 0), iota((side, small), 1)
    t1 = mm(mpo[...], one_hot(col_s * width + col_m == code_c)).astype(BF16)
    t2 = mm(one_hot(row_w * width + row_k == code_r), mpo[...]).astype(BF16)
    both = jnp.zeros((side, side), F32)
    for n in range(width):
        near = mm(one_hot(row_u * width + n == code_r), t1)
        both += near * mm(t2, one_hot(col_v * width + n == code_c))
    pair[...] = both.astype(BF16)

    cut_s = phys // 2
    lo, hi = pl.ds(0, cut_s), pl.ds(cut_s, phys - cut_s)
    arrive("site_x", site.at[:, block(bx), :], to_x)
    send("site_xy", site.at[lo, block(bx), :], site.at[lo, block(bx), :], to_y)
    arrive("site_y", site.at[:, block(by), :], to_y)
    send("site_yx", site.at[hi, block(by), :], site.at[hi, block(by), :], to_x)
    spread(0)
    loads["left"].wait()
    site_here.wait()
    arrive("site_xy", site.at[lo, block(bd), :], to_y)
    arrive("site_yx", site.at[hi, block(bd), :], to_x)

    strip = group * width

    @pl.loop(0, rows // group)
    def _(g):
        ours = left[pl.ds(pl.multiple_of(g * group, group), group)].astype(F32)
        ours = ours.reshape(strip, chi).astype(BF16)
        first = jnp.concatenate([mm(ours, site[s]).astype(BF16) for s in range(phys)], axis=0)
        out = mm(mix[...], first).astype(BF16)
        for u in range(phys):
            for n in range(width):
                at = (u * width + n) * group
                where = pl.multiple_of(u * rows + g * group, group)
                second[n, pl.ds(where, group), :] = out[at:at + group, :]

    half_w = width // 2
    order = [k + d * half_w for k in range(half_w) for d in range(2)]

    def first_round(n):
        if n < half_w:
            send(("rs_own", n), part.at[n, block(bx), :], rs1.at[n, 0], to_x)
            send(("rs_far", n), part.at[n, block(bd), :], rs1.at[n, 1], to_x)
        else:
            send(("rs_own", n), part.at[n, block(by), :], rs1.at[n, 0], to_y)
            send(("rs_far", n), part.at[n, block(bd), :], rs1.at[n, 1], to_y)

    behind = None
    for n in order:
        part[n] = mm(site_tr[...], second[n]).astype(BF16)
        if behind is not None:
            first_round(behind)
        behind = n
    first_round(behind)

    def second_round(n):
        if n < half_w:
            send(("rs_last", n), send2.at[n], rs2.at[n], to_y)
        else:
            send(("rs_last", n), send2.at[n], rs2.at[n], to_x)

    behind = None
    for n in order:
        src, other = (to_x, by) if n < half_w else (to_y, bx)
        arrive(("rs_far", n), rs1.at[n, 1], src)
        send2[n] = (part[n, block(other), :].astype(F32) + rs1[n, 1].astype(F32)).astype(BF16)
        if behind is not None:
            second_round(behind)
        behind = n
    second_round(behind)
    relay(0)
    spread(1)
    for n in order:
        src, last = (to_x, to_y) if n < half_w else (to_y, to_x)
        arrive(("rs_own", n), rs1.at[n, 0], src)
        arrive(("rs_last", n), rs2.at[n], last)
        total = part[n, block(me), :].astype(F32) + rs1[n, 0].astype(F32) + rs2[n].astype(F32)
        for i in range(cuts):
            acc[i, pl.ds(n, rows, stride=width), :] = total[:, i * lanes:(i + 1) * lanes]
    whole = jnp.concatenate([acc[i, :rows * width, :] for i in range(cuts)], axis=1)
    nl_own[...] = whole.astype(BF16)
    new_left[...] = whole.reshape(rows, width, chi).astype(BF16)
    send("left", nl_own, nl_in, to_next)
    relay(1)
    spread(2)
    loads["right"].wait()
    arrive("left", nl_in, to_next)

    for q in range(cuts):
        complete(q)

        def strip_of(g):
            high = batch * width
            ours = nl_in[pl.ds(pl.multiple_of(g * high, high), high), :]

            @pl.loop(0, pq // 2)
            def _(t):
                mixed[t] = mm(ours, psi[q, t])

            @pl.loop(0, batch // 2, unroll=4)
            def _(p):
                here = mixed[:, pl.ds(pl.multiple_of(p * 2 * width, 2 * width), 2 * width), :]
                tiles = []
                for i in range(2):
                    one = here[:, i * width:(i + 1) * width, :].reshape(pq // 2 * width, 2 * lanes)
                    tiles.append(jnp.concatenate([one[:, :lanes], one[:, lanes:]], axis=0))
                both = jnp.concatenate(tiles, axis=1).astype(BF16)
                out = mm(pair[...], both).astype(BF16)
                for i in range(2):
                    where = pl.ds(pl.multiple_of((p * 2 + i) * pq, pq), pq)
                    for k in range(width):
                        piece = out[k * pq:(k + 1) * pq, i * lanes:(i + 1) * lanes]
                        proj[where, k * lanes:(k + 1) * lanes] = piece

            env = right[:, q * lanes:(q + 1) * lanes, :].reshape(width * lanes, chi)
            total = mm(proj[...], env)
            long = pl.ds(pl.multiple_of(g * batch * pq, batch * pq), batch * pq)
            if q > 0:
                total += jnp.concatenate([acc[i, long, :] for i in range(cuts)], axis=1)
            if q < cuts - 1:
                for i in range(cuts):
                    acc[i, long, :] = total[:, i * lanes:(i + 1) * lanes]
            else:
                out = total.reshape(batch, phys, phys, chi).astype(BF16)
                product[pl.ds(pl.multiple_of(g * batch, batch), batch)] = out

        if 0 < q < cuts - 1:
            strip_of(0)
            relay(q + 1)
            if q + 2 < cuts:
                spread(q + 2)
            pl.loop(1, rows // batch)(strip_of)
        else:
            pl.loop(0, rows // batch)(strip_of)

    for copy in started:
        copy.wait_send()


def fused(left_env, site, psi, right_env, mpo):
    _, rows, width, chi = left_env.shape
    phys = site.shape[2]
    pq = phys * phys
    group, cuts, batch = 16, 4, 64
    lanes = chi // cuts
    small = phys * width
    table = mpo.transpose(3, 1, 2, 0).reshape(small, small)
    n_sems = 80
    any_spec = pl.BlockSpec(memory_space=pl.ANY)
    vmem = pl.BlockSpec(memory_space=pltpu.VMEM)
    new_left, product = pl.pallas_call(
        functools.partial(kernel, (rows, width, phys, chi, group, cuts, batch)),
        out_shape=(
            jax.ShapeDtypeStruct((rows, width, chi), BF16),
            jax.ShapeDtypeStruct((rows, phys, phys, chi), BF16),
        ),
        in_specs=[any_spec] * 5,
        out_specs=(vmem, vmem),
        scratch_shapes=[
            pltpu.VMEM((rows, width, chi), BF16),
            pltpu.VMEM((rows, phys, chi), BF16),
            pltpu.VMEM((rows, phys, phys, chi), BF16),
            pltpu.VMEM((small, small), BF16),
            pltpu.VMEM((width, chi, chi), BF16),
            pltpu.VMEM((phys, rows, chi), BF16),
            pltpu.VMEM((cuts, pq // 2, rows, 2 * lanes), BF16),
            pltpu.VMEM((phys, chi, chi), BF16),
            pltpu.VMEM((chi, phys * rows), BF16),
            pltpu.VMEM((small * group, small * group), BF16),
            pltpu.VMEM((width * pq, width * pq), BF16),
            pltpu.VMEM((width, phys * rows, chi), BF16),
            pltpu.VMEM((width, chi, chi), BF16),
            pltpu.VMEM((width, 2, rows, chi), BF16),
            pltpu.VMEM((width, rows, chi), BF16),
            pltpu.VMEM((width, rows, chi), BF16),
            pltpu.VMEM((rows * width, chi), BF16),
            pltpu.VMEM((rows * width, chi), BF16),
            pltpu.VMEM((cuts, pq // 2, chi, 2 * lanes), BF16),
            pltpu.VMEM((pq // 2, batch * width, 2 * lanes), F32),
            pltpu.VMEM((batch * pq, width * lanes), BF16),
            pltpu.VMEM((cuts, rows * pq, lanes), F32),
            pltpu.SemaphoreType.DMA((6,)),
            pltpu.SemaphoreType.DMA((n_sems,)),
            pltpu.SemaphoreType.DMA((n_sems,)),
        ],
        compiler_params=pltpu.CompilerParams(
            collective_id=0, has_side_effects=True, vmem_limit_bytes=62 * 1024 * 1024
        ),
    )(left_env[0], site[0], psi[0], right_env[0], table)
    return new_left[None], product[None]


def shifted(block, axis, distance):
    devices = range(lax.axis_size(axis))
    route = [((i - distance) % len(devices), i) for i in devices]
    return lax.ppermute(block, axis, route)


def shards(left_env, site, psi, right_env, mpo):
    left = left_env[0]
    tensor = site[0]
    rows = tensor.shape[0]
    phys = tensor.shape[1]
    chi = tensor.shape[2]
    width = left.shape[1]
    pair_source = shifted(psi[0], "sec", 1)
    offset = lax.axis_index("bond") * rows
    whole_left, whole_site = (
        lax.all_gather(left, "bond", axis=0, tiled=True),
        lax.all_gather(tensor, "bond", axis=0, tiled=True),
    )
    own_cols = lax.dynamic_slice_in_dim(whole_site, offset, rows, 2)
    first = jnp.dot(
        whole_left.reshape(chi * width, chi),
        own_cols.reshape(chi, phys * rows),
        preferred_element_type=jnp.float32,
    )
    first = first.astype(jnp.bfloat16).reshape(chi, width, phys, rows)
    second = jnp.einsum("pmsb,mnsu->punb", first, mpo, preferred_element_type=jnp.float32).astype(
        jnp.bfloat16
    )
    fresh = lax.dot_general(
        whole_site.reshape(chi * phys, chi),
        second.reshape(chi * phys, width * rows),
        (((0,), (0,)), ((), ())),
        preferred_element_type=jnp.float32,
    )
    fresh = fresh.astype(jnp.bfloat16).reshape(chi, width, rows)
    new_left = lax.all_to_all(fresh, "bond", split_axis=0, concat_axis=2, tiled=True)
    left_source = shifted(new_left, "sec", 1)
    source_flat = left_source.reshape(rows * width, chi)
    pair = pair_source.reshape(rows, phys * phys * chi)
    mixed = jnp.dot(
        source_flat,
        lax.all_gather(pair, "bond", axis=0, tiled=True),
        preferred_element_type=jnp.float32,
    )
    mixed = mixed.astype(jnp.bfloat16).reshape(rows, width * phys * phys, chi)
    two_site = jnp.einsum("mnsu,nkvw->msvuwk", mpo, mpo, preferred_element_type=jnp.float32)
    two_site = two_site.astype(jnp.bfloat16).reshape(width * phys * phys, phys * phys * width)
    projected = jnp.einsum(
        "pqc,qr->prc", mixed, two_site, preferred_element_type=jnp.float32
    ).astype(jnp.bfloat16)
    env_right = right_env[0].reshape(width * chi, chi)
    result = jnp.dot(
        projected.reshape(rows * phys * phys, width * chi),
        env_right,
        preferred_element_type=jnp.float32,
    ).astype(jnp.bfloat16)
    return (new_left[None], result.reshape(1, rows, phys, phys, chi))


def solution(mesh):
    in_specs = (
        P("sec", "bond", None, None),
        P("sec", "bond", None, None),
        P("sec", "bond", None, None, None),
        P("sec", None, None, None),
        P(),
    )
    out_specs = (P("sec", "bond", None, None), P("sec", "bond", None, None, None))
    body = fused if mesh.shape["bond"] == 4 else shards
    return jax.shard_map(body, mesh=mesh, in_specs=in_specs, out_specs=out_specs, check_vma=False)
```

profile of v0, /device:TPU:11, one launch (start us, length us, event | category | flops | bytes accessed | tf_op | source)
XLA Modules:
  0.0 145.1 jit_solution(18384994671334635302)
XLA Ops:
  0.6 0.9 copy.7
  1.5 0.7 reshape.7.mpo_h
  2.2 139.1 %shard_map.68 = (bf16[128,8,512]{2,1,0:T(8,128)(2,1)}, bf16[128,4,4,512]{3,2,1,0:T(4,128)(2,1)}) custom-call(bf16[128,8,512]{2,1,0:T(8,128)(2,1)} %bitcast.10, bf16[128,4,512]{2,1,0:T(4,128)(2,1)} %bitcast.12, bf16[128,4,4,512]{3,2,1,0:T(4,128)(2,1)} %bitcast.8, bf16[8,512,512]{2,1,0:T(8,128)(2,1)} %bitcast.7, bf16[32,32]{1,0:T(8,128)(2,1)} %reshape.7.mpo_h), custom_call_target="tpu_custom_call" | custom-call | tf_op jit(solution)/shard_map/pallas_call | solution.py:317
  141.3 0.0 copy-start
  141.4 2.4 %copy.10 = bf16[1,128,8,512]{3,2,1,0:T(8,128)(2,1)} copy(bf16[1,128,8,512]{3,2,1,0:T(8,128)(2,1)} %bitcast.11) | data formatting | bytes 2097152
  143.8 0.0 copy-done
  143.8 1.3 copy.11
Async XLA Ops:
  141.3 2.4 %copy-start = (bf16[128,4,4,512]{3,2,1,0:T(4,128)(2,1)S(1)}, bf16[128,4,4,512]{3,2,1,0:T(4,128)(2,1)}, u32[]{:S(2)}) copy-start(bf16[128,4,4,512]{3,2,1,0:T(4,128)(2,1)} %get-tuple-element.5) | copy-start | bytes 6291460
where the time goes:
time: 148 us; the launch traced here: 145 us
  Pallas kernels  139 us (94%)
  local copies, waits for them, and re-layouts  5.3 us (4%)
    pallas_call x1, Pallas kernels, fused(): pl.pallas_call(functools.partial(kernel, (rows, width, phys, chi, group,...  139 us
    unnamed x4, local copies, waits for them, and re-layouts  3.73 us

commit v1 on v0

v1 whole, which is shorter than its diff:
```python
import functools

import jax
import jax.numpy as jnp
from jax import lax
from jax.experimental import pallas as pl
from jax.experimental.pallas import tpu as pltpu
from jax.sharding import PartitionSpec as P

MESH = pl.DeviceIdType.MESH
BF16 = jnp.bfloat16
F32 = jnp.float32


def mm(a, b):
    return jnp.dot(a, b, preferred_element_type=F32)


def kernel(
    dims,
    left_h, site_h, psi_h, right_h, mpo_h,
    new_left, product,
    left, site_raw, psi_raw, mpo, right,
    site_own, psi_own, site, site_tr, mix, pair,
    second, part, rs1, send2, rs2, nl_own, nl_out, nl_in, psi, mixed, proj, prod, acc,
    local_sem, send_sem, recv_sem,
):
    rows, width, phys, chi, group, cuts, batch = dims
    pq = phys * phys
    n_sec = lax.axis_size("sec")
    sec = lax.axis_index("sec")
    me = lax.axis_index("bond")
    x, y = lax.rem(me, 2), me // 2
    core, z = lax.rem(sec, 2), sec // 2
    mate_sec = 2 * z + 1 - core
    side_bond = 2 * y + 1 - x
    to_c = {"sec": mate_sec}
    to_y = {"bond": 2 * (1 - y) + x}
    to_x = {"bond": side_bond}
    to_xc = {"sec": mate_sec, "bond": side_bond}
    up = lax.rem(sec + 2, n_sec)
    to_up = {"sec": up}
    stays = x == core
    moves = x != core
    shifts = x == 1
    rests = x == 0

    mine = 2 * y + core
    mates = 2 * y + 1 - core
    across = 2 * (1 - y) + core
    corner = 2 * (1 - y) + 1 - core

    def block(owner):
        return pl.ds(pl.multiple_of(owner * rows, rows), rows)

    loads = {}
    for i, (name, src, dst) in enumerate((
        ("site", site_h, site_raw),
        ("psi", psi_h, psi_raw),
        ("mpo", mpo_h, mpo),
    )):
        loads[name] = pltpu.make_async_copy(src, dst, local_sem.at[i])
        loads[name].start()

    barrier = pltpu.get_barrier_semaphore()
    greeted = [to_c, to_y, to_x, to_xc]
    for dz in (2, n_sec - 2):
        greeted.append({"sec": lax.rem(sec + dz, n_sec)})
        greeted.append({"sec": lax.rem(mate_sec + dz, n_sec), "bond": side_bond})
    for target in greeted:
        pl.semaphore_signal(barrier, inc=1, device_id=target, device_id_type=MESH)
    pl.semaphore_wait(barrier, len(greeted))

    started = {}
    counter = {}

    def slot(key):
        return counter.setdefault(key, len(counter))

    def remote(i, j, src, dst, target):
        return pltpu.make_async_remote_copy(
            src_ref=src, dst_ref=dst, send_sem=send_sem.at[i], recv_sem=recv_sem.at[j],
            device_id=target, device_id_type=MESH,
        )

    def send(key, src, dst, target, when=None, land=None):
        i = slot(key)
        copy = remote(i, i if land is None else land, src, dst, target)
        if when is None:
            copy.start()
        else:
            pl.when(when)(copy.start)
        started.setdefault(key, []).append((copy, when))

    def keep(key, src, dst, when, land=None):
        copy = pltpu.make_async_copy(src, dst, recv_sem.at[slot(key) if land is None else land])
        pl.when(when)(copy.start)

    def arrive(key, dst, land=None):
        i = slot(key)
        remote(i, i if land is None else land, dst, dst, to_c).wait_recv()

    lanes = chi // cuts
    halves = (pl.ds(0, phys // 2), pl.ds(phys // 2, phys - phys // 2))
    n_left = 4
    tall_left = rows // n_left

    def left_part(i):
        return pl.ds(i * tall_left, tall_left)

    def send_left(i):
        send(("left", i), left_h.at[left_part(i)], left.at[left_part(i)], to_xc, when=moves)
        keep(("left", i), left_h.at[left_part(i)], left.at[left_part(i)], stays)

    loads["site"].wait()
    flat = site_raw[...].astype(F32).reshape(rows * phys, chi)
    for i in range(cuts):
        acc[i, :rows * phys, :] = flat[:, i * lanes:(i + 1) * lanes]
    for t in range(phys):
        for i in range(cuts):
            tile = acc[i, pl.ds(t, rows, stride=phys), :]
            site_own[t, :, i * lanes:(i + 1) * lanes] = tile.astype(BF16)

    def site_spread(p, from_own):
        src = site_own.at[halves[p]] if from_own else site.at[halves[p], block(mine), :]
        when = stays if from_own else None
        send(("site_y", p), src, site.at[halves[p], block(mine), :], to_y, when)
        send(("site_c", p), src, site.at[halves[p], block(mine), :], to_c, when)

    for p in range(2):
        send(("site", p), site_own.at[halves[p]], site.at[halves[p], block(me), :], to_xc, when=moves)
        keep(("site", p), site_own.at[halves[p]], site.at[halves[p], block(me), :], stays)
        site_spread(p, True)
    for i in range(n_left):
        send_left(i)

    loads["psi"].wait()
    tall = 8

    @pl.loop(0, rows // tall)
    def _(g):
        flat = psi_raw[pl.ds(pl.multiple_of(g * tall, tall), tall)].astype(F32)
        flat = flat.reshape(tall * pq, chi)
        where = pl.ds(pl.multiple_of(g * tall * pq, tall * pq), tall * pq)
        for i in range(cuts):
            acc[i, where, :] = flat[:, i * lanes:(i + 1) * lanes]

    def region(q, owner):
        return psi.at[q, :, block(owner), :]

    psi_self = jnp.logical_and(x == 0, core == 0)
    psi_goes = jnp.logical_not(psi_self)
    to_psi = {
        "sec": lax.rem(2 * z + x + 2 * core, n_sec),
        "bond": 2 * y + core,
    }

    def launch(q):
        send(("own", q), psi_own.at[q], region(q, me), to_psi, when=psi_goes)
        keep(("own", q), psi_own.at[q], region(q, me), psi_self)

    for q in range(cuts):
        for t in range(pq):
            at = (t % 2) * lanes
            tile = acc[q, pl.ds(t, rows, stride=pq), :]
            psi_own[q, t // 2, :, at:at + lanes] = tile.astype(BF16)
        if 0 < q < 3:
            launch(q - 1)

    send("right", right_h, right, to_c, when=moves)
    keep("right", right_h, right, moves)

    def spread(q):
        arrive(("own", q), region(q, mine))
        send(("psi_y", q), region(q, mine), region(q, mine), to_y)
        send(("psi_c", q), region(q, mine), region(q, mine), to_c)

    def relay(q):
        arrive(("psi_y", q), region(q, across))
        send(("psi_yc", q), region(q, across), region(q, across), to_c)

    def complete(q):
        arrive(("psi_c", q), region(q, mates))
        arrive(("psi_yc", q), region(q, corner))

    @pl.when(moves)
    def _():
        for p in range(2):
            arrive(("site", p), site.at[halves[p], block(mine), :])
            src = site.at[halves[p], block(mine), :]
            remote(slot(("site_y", p)), slot(("site_y", p)), src, src, to_y).start()
            remote(slot(("site_c", p)), slot(("site_c", p)), src, src, to_c).start()

    @pl.when(stays)
    def _():
        for p in range(2):
            arrive(("site", p), site.at[halves[p], block(mine), :])

    for p in range(2):
        for key, target in (("site_y", to_y), ("site_c", to_c)):
            src = site.at[halves[p], block(mine), :]
            i = slot((key, p))
            started[(key, p)] = [(remote(i, i, src, src, target), None)]

    loads["mpo"].wait()

    def iota(shape, axis):
        return lax.broadcasted_iota(jnp.int32, shape, axis)

    def one_hot(condition):
        return jnp.where(condition, 1.0, 0.0).astype(BF16)

    small = phys * width
    big = small * group
    tall_code = lax.div(iota((big, small), 0), group)
    spread_rows = one_hot(tall_code == iota((big, small), 1))
    col = iota((small, big), 1)
    col_code = lax.div(col, group * width) * width + lax.rem(col, width)
    spread_cols = one_hot(col_code == iota((small, big), 0))
    wide = mm(mm(spread_rows, mpo[...]).astype(BF16), spread_cols)
    same = lax.rem(iota((big, big), 0), group) == lax.rem(lax.div(iota((big, big), 1), width), group)
    mix[...] = jnp.where(same, wide, 0.0).astype(BF16)

    for t in range(phys):
        own = site[t, block(mine), :].astype(F32)
        for i in range(cuts):
            tile = own[:, i * lanes:(i + 1) * lanes]
            site_tr[i * lanes:(i + 1) * lanes, t * rows:(t + 1) * rows] = tile.T.astype(BF16)

    for p in range(2):
        arrive(("site_y", p), site.at[halves[p], block(across), :])
        send(("site_yc", p), site.at[halves[p], block(across), :], site.at[halves[p], block(across), :], to_c)

    def early(q):
        @pl.when(stays)
        def _():
            arrive(("own", q), region(q, mine))
            for key, target in (("psi_y", to_y), ("psi_c", to_c)):
                i = slot((key, q))
                remote(i, i, region(q, mine), region(q, mine), target).start()

    def late(q):
        @pl.when(moves)
        def _():
            arrive(("own", q), region(q, mine))
            for key, target in (("psi_y", to_y), ("psi_c", to_c)):
                i = slot((key, q))
                remote(i, i, region(q, mine), region(q, mine), target).start()
        for key, target in (("psi_y", to_y), ("psi_c", to_c)):
            i = slot((key, q))
            started[(key, q)] = [(remote(i, i, region(q, mine), region(q, mine), target), None)]

    early(0)
    for p in range(2):
        arrive(("site_c", p), site.at[halves[p], block(mates), :])
        arrive(("site_yc", p), site.at[halves[p], block(corner), :])

    strip = group * width
    per_left = tall_left // group

    for i in range(n_left):
        arrive(("left", i), left.at[left_part(i)])

        @pl.loop(i * per_left, (i + 1) * per_left)
        def _(g):
            ours = left[pl.ds(pl.multiple_of(g * group, group), group)].astype(F32)
            ours = ours.reshape(strip, chi).astype(BF16)
            first = jnp.concatenate([mm(ours, site[s]).astype(BF16) for s in range(phys)], axis=0)
            out = mm(mix[...], first).astype(BF16)
            for u in range(phys):
                for n in range(width):
                    at = (u * width + n) * group
                    where = pl.multiple_of(u * rows + g * group, group)
                    second[n, pl.ds(where, group), :] = out[at:at + group, :]

        if i == 1:
            early(1)

    launch(2)

    hrows = rows // 2

    def rows_of(stage, far, half):
        yy = 1 - y if far else y
        column = 1 - x if stage == 0 else x
        start = (2 * yy + column) * rows + half * hrows
        return pl.ds(pl.multiple_of(start, hrows), hrows)

    def block_of(stage, far):
        yy = 1 - y if far else y
        column = 1 - x if stage == 0 else x
        return block(2 * yy + column)

    def partial(stage):
        for far in (1, 0):
            where = block_of(stage, far)
            for n in range(width):
                part[n, where, :] = mm(site_tr[where, :], second[n]).astype(BF16)

    def swap_halves(stage):
        for far in (1, 0):
            send(("rs1", stage, far), part.at[:, rows_of(stage, far, 1 - core), :], rs1.at[stage, far], to_c)

    n_rs = 4
    rs_rows = hrows // n_rs

    def add_far(stage):
        arrive(("rs1", stage, 1), rs1.at[stage, 1])
        for n in range(width):
            total = part[n, rows_of(stage, 1, core), :].astype(F32) + rs1[stage, 1, n].astype(F32)
            send2[stage, n] = total.astype(BF16)

    def send_far(stage):
        for j in range(n_rs):
            where = pl.ds(j * rs_rows, rs_rows)
            send(("rs2", stage, j), send2.at[stage, :, where, :], rs2.at[stage, :, where, :], to_y)

    def finish(stage):
        arrive(("rs1", stage, 0), rs1.at[stage, 0])
        base = stage * hrows * width
        for j in range(n_rs):
            where = pl.ds(j * rs_rows, rs_rows)
            arrive(("rs2", stage, j), rs2.at[stage, :, where, :])
            yy = y
            column = 1 - x if stage == 0 else x
            start = (2 * yy + column) * rows + core * hrows + j * rs_rows
            near = pl.ds(pl.multiple_of(start, rs_rows), rs_rows)
            for n in range(width):
                total = part[n, near, :].astype(F32) + rs1[stage, 0, n, where, :].astype(F32)
                total += rs2[stage, n, where, :].astype(F32)
                for i in range(cuts):
                    acc[i, pl.ds(base + j * rs_rows * width + n, rs_rows, stride=width), :] = (
                        total[:, i * lanes:(i + 1) * lanes])
            high = pl.ds(j * rs_rows * width, rs_rows * width)
            whole = jnp.concatenate(
                [acc[i, pl.ds(base + j * rs_rows * width, rs_rows * width), :] for i in range(cuts)], axis=1)
            nl_own[stage, high, :] = whole.astype(BF16)
            nl_out[stage, where] = whole.reshape(rs_rows, width, chi).astype(BF16)
            send(("up", stage, j), nl_own.at[stage, high, :], nl_in.at[stage, high, :], to_up, when=shifts)
            keep(("up", stage, j), nl_own.at[stage, high, :], nl_in.at[stage, high, :], rests)

    my_half = pl.ds(pl.multiple_of(core * hrows, hrows), hrows)
    mate_half = pl.ds(pl.multiple_of((1 - core) * hrows, hrows), hrows)
    nl_slots = [slot(("nl_land", h)) for h in range(2)]
    assert nl_slots[1] == nl_slots[0] + 1
    nl_land = nl_slots[0] + core
    n_out = 4
    out_slots = [[slot(("out_land", h, j)) for j in range(n_out)] for h in range(2)]
    out_rows = hrows // n_out

    def home_left(stage):
        src, dst = nl_out.at[stage], new_left.at[my_half]
        if stage == 0:
            send(("nl0", 0), src, dst, to_x, when=stays, land=nl_land)
            send(("nl0", 1), src, dst, to_xc, when=moves, land=nl_land)
        else:
            send(("nl1", 0), src, dst, to_c, when=moves, land=nl_land)
            keep(("nl1", 1), src, dst, stays, land=nl_land)

    def home_product(stage, j):
        start = core * hrows + j * out_rows
        dst = product.at[pl.ds(pl.multiple_of(start, out_rows), out_rows)]
        src = prod.at[stage, pl.ds(j * out_rows, out_rows)]
        land = out_slots[0][j] + core * n_out
        if stage == 0:
            send(("out0", j, 0), src, dst, to_xc, when=stays, land=land)
            send(("out0", j, 1), src, dst, to_x, when=moves, land=land)
        else:
            send(("out1", j, 0), src, dst, to_c, when=stays, land=land)
            keep(("out1", j, 1), src, dst, moves, land=land)

    partial(0)
    swap_halves(0)
    partial(1)
    add_far(0)
    swap_halves(1)
    send_far(0)
    late(0)
    launch(3)

    side = width * pq
    col = iota((small, side), 1)
    col_m = lax.rem(col, width)
    col_sv = lax.rem(lax.div(col, width), pq // 2) * 2 + lax.div(col, width * (pq // 2))
    col_s, col_v = lax.div(col_sv, phys), lax.rem(col_sv, phys)
    row = iota((side, small), 0)
    row_k, row_u, row_w = lax.div(row, pq), lax.rem(lax.div(row, phys), phys), lax.rem(row, phys)
    code_c, code_r = iota((small, side), 0), iota((side, small), 1)
    t1 = mm(mpo[...], one_hot(col_s * width + col_m == code_c)).astype(BF16)
    t2 = mm(one_hot(row_w * width + row_k == code_r), mpo[...]).astype(BF16)
    both = jnp.zeros((side, side), F32)
    for n in range(width):
        near = mm(one_hot(row_u * width + n == code_r), t1)
        both += near * mm(t2, one_hot(col_v * width + n == code_c))
    pair[...] = both.astype(BF16)

    add_far(1)
    late(1)
    finish(0)
    home_left(0)
    relay(0)
    spread(2)
    arrive("right", right)

    def strip_of(stage, q):
        ours = nl_in[stage]

        @pl.loop(0, pq // 2)
        def _(t):
            mixed[t] = mm(ours, psi[q, t])

        @pl.loop(0, batch // 2, unroll=4)
        def _(p):
            here = mixed[:, pl.ds(pl.multiple_of(p * 2 * width, 2 * width), 2 * width), :]
            tiles = []
            for i in range(2):
                one = here[:, i * width:(i + 1) * width, :].reshape(pq // 2 * width, 2 * lanes)
                tiles.append(jnp.concatenate([one[:, :lanes], one[:, lanes:]], axis=0))
            both = jnp.concatenate(tiles, axis=1).astype(BF16)
            out = mm(pair[...], both).astype(BF16)
            for i in range(2):
                where = pl.ds(pl.multiple_of((p * 2 + i) * pq, pq), pq)
                for k in range(width):
                    piece = out[k * pq:(k + 1) * pq, i * lanes:(i + 1) * lanes]
                    proj[where, k * lanes:(k + 1) * lanes] = piece

        env = right[:, q * lanes:(q + 1) * lanes, :].reshape(width * lanes, chi)
        high = out_rows * pq
        for j in range(n_out):
            total = mm(proj[j * high:(j + 1) * high, :], env)
            long = pl.ds(stage * batch * pq + j * high, high)
            if q > 0:
                total += jnp.concatenate([acc[i, long, :] for i in range(cuts)], axis=1)
            if q < cuts - 1:
                for i in range(cuts):
                    acc[i, long, :] = total[:, i * lanes:(i + 1) * lanes]
            else:
                out = total.reshape(out_rows, phys, phys, chi).astype(BF16)
                prod[stage, j * out_rows:(j + 1) * out_rows] = out
                home_product(stage, j)

    complete(0)
    for j in range(n_rs):
        high = pl.ds(j * rs_rows * width, rs_rows * width)
        arrive(("up", 0, j), nl_in.at[0, high, :])
    strip_of(0, 0)
    relay(1)
    spread(3)
    send_far(1)
    complete(1)
    strip_of(0, 1)
    relay(2)
    complete(2)
    strip_of(0, 2)
    relay(3)
    complete(3)
    strip_of(0, 3)
    finish(1)
    home_left(1)
    for j in range(n_rs):
        high = pl.ds(j * rs_rows * width, rs_rows * width)
        arrive(("up", 1, j), nl_in.at[1, high, :])
    for q in range(cuts):
        strip_of(1, q)

    for h in range(2):
        where = pl.ds(h * hrows, hrows)
        arrive(("nl_land", h), new_left.at[where])
        for j in range(n_out):
            arrive(("out_land", h, j), product.at[pl.ds(h * hrows + j * out_rows, out_rows)])
    for copies in started.values():
        for copy, when in copies:
            if when is None:
                copy.wait_send()
            else:
                pl.when(when)(copy.wait_send)


def fused(left_env, site, psi, right_env, mpo):
    _, rows, width, chi = left_env.shape
    phys = site.shape[2]
    pq = phys * phys
    group, cuts, batch = 16, 4, rows // 2
    lanes = chi // cuts
    small = phys * width
    table = mpo.transpose(3, 1, 2, 0).reshape(small, small)
    n_sems = 120
    any_spec = pl.BlockSpec(memory_space=pl.ANY)
    vmem = pl.BlockSpec(memory_space=pltpu.VMEM)
    new_left, product = pl.pallas_call(
        functools.partial(kernel, (rows, width, phys, chi, group, cuts, batch)),
        out_shape=(
            jax.ShapeDtypeStruct((rows, width, chi), BF16),
            jax.ShapeDtypeStruct((rows, phys, phys, chi), BF16),
        ),
        in_specs=[any_spec] * 5,
        out_specs=(vmem, vmem),
        scratch_shapes=[
            pltpu.VMEM((rows, width, chi), BF16),
            pltpu.VMEM((rows, phys, chi), BF16),
            pltpu.VMEM((rows, phys, phys, chi), BF16),
            pltpu.VMEM((small, small), BF16),
            pltpu.VMEM((width, chi, chi), BF16),
            pltpu.VMEM((phys, rows, chi), BF16),
            pltpu.VMEM((cuts, pq // 2, rows, 2 * lanes), BF16),
            pltpu.VMEM((phys, chi, chi), BF16),
            pltpu.VMEM((chi, phys * rows), BF16),
            pltpu.VMEM((small * group, small * group), BF16),
            pltpu.VMEM((width * pq, width * pq), BF16),
            pltpu.VMEM((width, phys * rows, chi), BF16),
            pltpu.VMEM((width, chi, chi), BF16),
            pltpu.VMEM((2, 2, width, rows // 2, chi), BF16),
            pltpu.VMEM((2, width, rows // 2, chi), BF16),
            pltpu.VMEM((2, width, rows // 2, chi), BF16),
            pltpu.VMEM((2, rows // 2 * width, chi), BF16),
            pltpu.VMEM((2, rows // 2, width, chi), BF16),
            pltpu.VMEM((2, rows // 2 * width, chi), BF16),
            pltpu.VMEM((cuts, pq // 2, chi, 2 * lanes), BF16),
            pltpu.VMEM((pq // 2, batch * width, 2 * lanes), F32),
            pltpu.VMEM((batch * pq, width * lanes), BF16),
            pltpu.VMEM((2, rows // 2, phys, phys, chi), BF16),
            pltpu.VMEM((cuts, rows * pq, lanes), F32),
            pltpu.SemaphoreType.DMA((6,)),
            pltpu.SemaphoreType.DMA((n_sems,)),
            pltpu.SemaphoreType.DMA((n_sems,)),
        ],
        compiler_params=pltpu.CompilerParams(
            collective_id=0, has_side_effects=True, vmem_limit_bytes=62 * 1024 * 1024
        ),
    )(left_env[0], site[0], psi[0], right_env[0], table)
    return new_left[None], product[None]


def shifted(block, axis, distance):
    devices = range(lax.axis_size(axis))
    route = [((i - distance) % len(devices), i) for i in devices]
    return lax.ppermute(block, axis, route)


def shards(left_env, site, psi, right_env, mpo):
    left = left_env[0]
    tensor = site[0]
    rows = tensor.shape[0]
    phys = tensor.shape[1]
    chi = tensor.shape[2]
    width = left.shape[1]
    pair_source = shifted(psi[0], "sec", 1)
    offset = lax.axis_index("bond") * rows
    whole_left, whole_site = (
        lax.all_gather(left, "bond", axis=0, tiled=True),
        lax.all_gather(tensor, "bond", axis=0, tiled=True),
    )
    own_cols = lax.dynamic_slice_in_dim(whole_site, offset, rows, 2)
    first = jnp.dot(
        whole_left.reshape(chi * width, chi),
        own_cols.reshape(chi, phys * rows),
        preferred_element_type=jnp.float32,
    )
    first = first.astype(jnp.bfloat16).reshape(chi, width, phys, rows)
    second = jnp.einsum("pmsb,mnsu->punb", first, mpo, preferred_element_type=jnp.float32).astype(
        jnp.bfloat16
    )
    fresh = lax.dot_general(
        whole_site.reshape(chi * phys, chi),
        second.reshape(chi * phys, width * rows),
        (((0,), (0,)), ((), ())),
        preferred_element_type=jnp.float32,
    )
    fresh = fresh.astype(jnp.bfloat16).reshape(chi, width, rows)
    new_left = lax.all_to_all(fresh, "bond", split_axis=0, concat_axis=2, tiled=True)
    left_source = shifted(new_left, "sec", 1)
    source_flat = left_source.reshape(rows * width, chi)
    pair = pair_source.reshape(rows, phys * phys * chi)
    mixed = jnp.dot(
        source_flat,
        lax.all_gather(pair, "bond", axis=0, tiled=True),
        preferred_element_type=jnp.float32,
    )
    mixed = mixed.astype(jnp.bfloat16).reshape(rows, width * phys * phys, chi)
    two_site = jnp.einsum("mnsu,nkvw->msvuwk", mpo, mpo, preferred_element_type=jnp.float32)
    two_site = two_site.astype(jnp.bfloat16).reshape(width * phys * phys, phys * phys * width)
    projected = jnp.einsum(
        "pqc,qr->prc", mixed, two_site, preferred_element_type=jnp.float32
    ).astype(jnp.bfloat16)
    env_right = right_env[0].reshape(width * chi, chi)
    result = jnp.dot(
        projected.reshape(rows * phys * phys, width * chi),
        env_right,
        preferred_element_type=jnp.float32,
    ).astype(jnp.bfloat16)
    return (new_left[None], result.reshape(1, rows, phys, phys, chi))


def solution(mesh):
    in_specs = (
        P("sec", "bond", None, None),
        P("sec", "bond", None, None),
        P("sec", "bond", None, None, None),
        P("sec", None, None, None),
        P(),
    )
    out_specs = (P("sec", "bond", None, None), P("sec", "bond", None, None, None))
    body = fused if mesh.shape["bond"] == 4 else shards
    return jax.shard_map(body, mesh=mesh, in_specs=in_specs, out_specs=out_specs, check_vma=False)
```

time: 148 us -> 156 us (1.054); the launches traced: 145 us -> 156 us
  Pallas kernels: 139 us -> 150 us
    pallas_call x1, Pallas kernels: 139 us -> 150 us  [fused(): pl.pallas_call(functools.partial(kernel, (rows, width, phys, chi, group,...]
where the time goes in v1:
time: 156 us
  Pallas kernels  150 us (96%)
  local copies, waits for them, and re-layouts  5.3 us (3%)
    pallas_call x1, Pallas kernels, fused(): pl.pallas_call(functools.partial(kernel, (rows, width, phys, chi, group,...  150 us
    unnamed x4, local copies, waits for them, and re-layouts  3.73 us

profile of v1, /device:TPU:11, one launch (start us, length us, event | category | flops | bytes accessed | tf_op | source)
XLA Modules:
  0.0 155.7 jit_solution(5630234576290990021)
XLA Ops:
  0.6 0.9 copy.7
  1.5 0.7 reshape.7.mpo_h
  2.2 149.7 %shard_map.68 = (bf16[128,8,512]{2,1,0:T(8,128)(2,1)}, bf16[128,4,4,512]{3,2,1,0:T(4,128)(2,1)}) custom-call(bf16[128,8,512]{2,1,0:T(8,128)(2,1)} %bitcast.10, bf16[128,4,512]{2,1,0:T(4,128)(2,1)} %bitcast.12, bf16[128,4,4,512]{3,2,1,0:T(4,128)(2,1)} %bitcast.8, bf16[8,512,512]{2,1,0:T(8,128)(2,1)} %bitcast.7, bf16[32,32]{1,0:T(8,128)(2,1)} %reshape.7.mpo_h), custom_call_target="tpu_custom_call" | custom-call | tf_op jit(solution)/shard_map/pallas_call | solution.py:490
  151.9 0.0 copy-start
  151.9 2.4 %copy.10 = bf16[1,128,8,512]{3,2,1,0:T(8,128)(2,1)} copy(bf16[1,128,8,512]{3,2,1,0:T(8,128)(2,1)} %bitcast.11) | data formatting | bytes 2097152
  154.3 0.0 copy-done
  154.3 1.3 copy.11
Async XLA Ops:
  151.9 2.4 %copy-start = (bf16[128,4,4,512]{3,2,1,0:T(4,128)(2,1)S(1)}, bf16[128,4,4,512]{3,2,1,0:T(4,128)(2,1)}, u32[]{:S(2)}) copy-start(bf16[128,4,4,512]{3,2,1,0:T(4,128)(2,1)} %get-tuple-element.5) | copy-start | bytes 6291460

commit v2 on v1

--- a/solution.py
+++ b/solution.py
@@ -73,6 +73,8 @@
 
     started = {}
     counter = {}
+    lands = {}
+    landed = set()
 
     def slot(key):
         return counter.setdefault(key, len(counter))
@@ -91,17 +93,19 @@
         else:
             pl.when(when)(copy.start)
         started.setdefault(key, []).append((copy, when))
+        lands[key] = dst
 
     def keep(key, src, dst, when, land=None):
         copy = pltpu.make_async_copy(src, dst, recv_sem.at[slot(key) if land is None else land])
         pl.when(when)(copy.start)
 
-    def arrive(key, dst, land=None):
+    def arrive(key, dst):
         i = slot(key)
-        remote(i, i if land is None else land, dst, dst, to_c).wait_recv()
+        landed.add(key)
+        remote(i, i, dst, dst, to_c).wait_recv()
 
     lanes = chi // cuts
-    halves = (pl.ds(0, phys // 2), pl.ds(phys // 2, phys - phys // 2))
+    pieces = tuple(pl.ds(t, 1) for t in range(phys))
     n_left = 4
     tall_left = rows // n_left
 
@@ -122,14 +126,14 @@
             site_own[t, :, i * lanes:(i + 1) * lanes] = tile.astype(BF16)
 
     def site_spread(p, from_own):
-        src = site_own.at[halves[p]] if from_own else site.at[halves[p], block(mine), :]
+        src = site_own.at[pieces[p]] if from_own else site.at[pieces[p], block(mine), :]
         when = stays if from_own else None
-        send(("site_y", p), src, site.at[halves[p], block(mine), :], to_y, when)
-        send(("site_c", p), src, site.at[halves[p], block(mine), :], to_c, when)
-
-    for p in range(2):
-        send(("site", p), site_own.at[halves[p]], site.at[halves[p], block(me), :], to_xc, when=moves)
-        keep(("site", p), site_own.at[halves[p]], site.at[halves[p], block(me), :], stays)
+        send(("site_y", p), src, site.at[pieces[p], block(mine), :], to_y, when)
+        send(("site_c", p), src, site.at[pieces[p], block(mine), :], to_c, when)
+
+    for p in range(phys):
+        send(("site", p), site_own.at[pieces[p]], site.at[pieces[p], block(me), :], to_xc, when=moves)
+        keep(("site", p), site_own.at[pieces[p]], site.at[pieces[p], block(me), :], stays)
         site_spread(p, True)
     for i in range(n_left):
         send_left(i)
@@ -149,31 +153,44 @@
         return psi.at[q, :, block(owner), :]
 
     psi_self = jnp.logical_and(x == 0, core == 0)
-    psi_goes = jnp.logical_not(psi_self)
     to_psi = {
         "sec": lax.rem(2 * z + x + 2 * core, n_sec),
         "bond": 2 * y + core,
     }
 
+    psi_waits = jnp.logical_and(x == 0, core == 1)
+    psi_now = x == 1
+
     def launch(q):
-        send(("own", q), psi_own.at[q], region(q, me), to_psi, when=psi_goes)
+        send(("own", q), psi_own.at[q], region(q, me), to_psi, when=psi_now)
         keep(("own", q), psi_own.at[q], region(q, me), psi_self)
+
+    def launch_late(q):
+        send(("own", q), psi_own.at[q], region(q, me), to_psi, when=psi_waits)
 
     for q in range(cuts):
         for t in range(pq):
             at = (t % 2) * lanes
             tile = acc[q, pl.ds(t, rows, stride=pq), :]
             psi_own[q, t // 2, :, at:at + lanes] = tile.astype(BF16)
-        if 0 < q < 3:
+        if q > 0:
             launch(q - 1)
-
-    send("right", right_h, right, to_c, when=moves)
-    keep("right", right_h, right, moves)
-
-    def spread(q):
-        arrive(("own", q), region(q, mine))
-        send(("psi_y", q), region(q, mine), region(q, mine), to_y)
-        send(("psi_c", q), region(q, mine), region(q, mine), to_c)
+    launch(cuts - 1)
+
+    def spread_if(q, when, last):
+        @pl.when(when)
+        def _():
+            arrive(("own", q), region(q, mine))
+            for key, target in (("psi_y", to_y), ("psi_c", to_c)):
+                i = slot((key, q))
+                remote(i, i, region(q, mine), region(q, mine), target).start()
+        if last:
+            for key, target in (("psi_y", to_y), ("psi_c", to_c)):
+                i = slot((key, q))
+                started[(key, q)] = [(remote(i, i, region(q, mine), region(q, mine), target), None)]
+                lands[(key, q)] = region(q, mine)
+
+    stays_up = jnp.logical_and(x == 1, core == 1)
 
     def relay(q):
         arrive(("psi_y", q), region(q, across))
@@ -183,22 +200,25 @@
         arrive(("psi_c", q), region(q, mates))
         arrive(("psi_yc", q), region(q, corner))
 
+    spread_if(0, psi_self, False)
+    spread_if(1, psi_self, False)
+
     @pl.when(moves)
     def _():
-        for p in range(2):
-            arrive(("site", p), site.at[halves[p], block(mine), :])
-            src = site.at[halves[p], block(mine), :]
+        for p in range(phys):
+            arrive(("site", p), site.at[pieces[p], block(mine), :])
+            src = site.at[pieces[p], block(mine), :]
             remote(slot(("site_y", p)), slot(("site_y", p)), src, src, to_y).start()
             remote(slot(("site_c", p)), slot(("site_c", p)), src, src, to_c).start()
 
     @pl.when(stays)
     def _():
-        for p in range(2):
-            arrive(("site", p), site.at[halves[p], block(mine), :])
-
-    for p in range(2):
+        for p in range(phys):
+            arrive(("site", p), site.at[pieces[p], block(mine), :])
+
+    for p in range(phys):
         for key, target in (("site_y", to_y), ("site_c", to_c)):
-            src = site.at[halves[p], block(mine), :]
+            src = site.at[pieces[p], block(mine), :]
             i = slot((key, p))
             started[(key, p)] = [(remote(i, i, src, src, target), None)]
 
@@ -227,34 +247,17 @@
             tile = own[:, i * lanes:(i + 1) * lanes]
             site_tr[i * lanes:(i + 1) * lanes, t * rows:(t + 1) * rows] = tile.T.astype(BF16)
 
-    for p in range(2):
-        arrive(("site_y", p), site.at[halves[p], block(across), :])
-        send(("site_yc", p), site.at[halves[p], block(across), :], site.at[halves[p], block(across), :], to_c)
-
-    def early(q):
-        @pl.when(stays)
-        def _():
-            arrive(("own", q), region(q, mine))
-            for key, target in (("psi_y", to_y), ("psi_c", to_c)):
-                i = slot((key, q))
-                remote(i, i, region(q, mine), region(q, mine), target).start()
-
-    def late(q):
-        @pl.when(moves)
-        def _():
-            arrive(("own", q), region(q, mine))
-            for key, target in (("psi_y", to_y), ("psi_c", to_c)):
-                i = slot((key, q))
-                remote(i, i, region(q, mine), region(q, mine), target).start()
-        for key, target in (("psi_y", to_y), ("psi_c", to_c)):
-            i = slot((key, q))
-            started[(key, q)] = [(remote(i, i, region(q, mine), region(q, mine), target), None)]
-
-    early(0)
-    for p in range(2):
-        arrive(("site_c", p), site.at[halves[p], block(mates), :])
-        arrive(("site_yc", p), site.at[halves[p], block(corner), :])
-
+    for p in range(phys):
+        arrive(("site_y", p), site.at[pieces[p], block(across), :])
+        send(("site_yc", p), site.at[pieces[p], block(across), :], site.at[pieces[p], block(across), :], to_c)
+
+    spread_if(0, stays_up, False)
+    for p in range(phys):
+        arrive(("site_c", p), site.at[pieces[p], block(mates), :])
+        arrive(("site_yc", p), site.at[pieces[p], block(corner), :])
+
+    send(("right",), right_h, right, to_c, when=moves)
+    keep(("right",), right_h, right, moves)
     strip = group * width
     per_left = tall_left // group
 
@@ -273,10 +276,12 @@
                     where = pl.multiple_of(u * rows + g * group, group)
                     second[n, pl.ds(where, group), :] = out[at:at + group, :]
 
-        if i == 1:
-            early(1)
-
-    launch(2)
+        if i == 0:
+            spread_if(1, stays_up, False)
+        if i == n_left - 2:
+            for q in range(cuts):
+                launch_late(q)
+
 
     hrows = rows // 2
 
@@ -369,14 +374,35 @@
             send(("out1", j, 0), src, dst, to_c, when=stays, land=land)
             keep(("out1", j, 1), src, dst, moves, land=land)
 
+    def finalize():
+        for key in list(started):
+            if key[0] not in ("nl0", "nl1", "out0", "out1") and key not in landed:
+                arrive(key, lands[key])
+        for h in range(2):
+            where = pl.ds(h * hrows, hrows)
+            for stage, when in ((0, moves), (1, stays)):
+                if (f"nl{stage}", 0) in started:
+                    pl.when(when)(functools.partial(arrive, ("nl_land", h), new_left.at[where]))
+            for stage, when in ((0, stays), (1, moves)):
+                for j in range(n_out):
+                    if (f"out{stage}", j, 0) in started:
+                        where = pl.ds(h * hrows + j * out_rows, out_rows)
+                        pl.when(when)(functools.partial(arrive, ("out_land", h, j), product.at[where]))
+        for copies in started.values():
+            for copy, when in copies:
+                if when is None:
+                    copy.wait_send()
+                else:
+                    pl.when(when)(copy.wait_send)
+
     partial(0)
     swap_halves(0)
     partial(1)
     add_far(0)
     swap_halves(1)
     send_far(0)
-    late(0)
-    launch(3)
+    spread_if(2, stays, False)
+    spread_if(0, moves, True)
 
     side = width * pq
     col = iota((small, side), 1)
@@ -395,12 +421,13 @@
     pair[...] = both.astype(BF16)
 
     add_far(1)
-    late(1)
+    spread_if(1, moves, True)
     finish(0)
     home_left(0)
+    spread_if(2, moves, True)
+    spread_if(3, stays, False)
     relay(0)
-    spread(2)
-    arrive("right", right)
+    arrive(("right",), right)
 
     def strip_of(stage, q):
         ours = nl_in[stage]
@@ -445,13 +472,13 @@
         arrive(("up", 0, j), nl_in.at[0, high, :])
     strip_of(0, 0)
     relay(1)
-    spread(3)
-    send_far(1)
+    spread_if(3, moves, True)
     complete(1)
     strip_of(0, 1)
     relay(2)
     complete(2)
     strip_of(0, 2)
+    send_far(1)
     relay(3)
     complete(3)
     strip_of(0, 3)
@@ -463,17 +490,7 @@
     for q in range(cuts):
         strip_of(1, q)
 
-    for h in range(2):
-        where = pl.ds(h * hrows, hrows)
-        arrive(("nl_land", h), new_left.at[where])
-        for j in range(n_out):
-            arrive(("out_land", h, j), product.at[pl.ds(h * hrows + j * out_rows, out_rows)])
-    for copies in started.values():
-        for copy, when in copies:
-            if when is None:
-                copy.wait_send()
-            else:
-                pl.when(when)(copy.wait_send)
+    finalize()
 
 
 def fused(left_env, site, psi, right_env, mpo):

time: 156 us -> 132 us (0.85)
  Pallas kernels: 150 us -> 126 us
    pallas_call x1, Pallas kernels: 150 us -> 126 us  [fused(): pl.pallas_call(functools.partial(kernel, (rows, width, phys, chi, group,...]
where the time goes in v2:
time: 132 us
  Pallas kernels  126 us (95%)
  local copies, waits for them, and re-layouts  5.3 us (4%)
    pallas_call x1, Pallas kernels, fused(): pl.pallas_call(functools.partial(kernel, (rows, width, phys, chi, group,...  126 us
    unnamed x4, local copies, waits for them, and re-layouts  3.73 us

profile of v2, /device:TPU:11, one launch (start us, length us, event | category | flops | bytes accessed | tf_op | source)
XLA Modules:
  0.0 132.0 jit_solution(4781544033879181503)
XLA Ops:
  0.6 0.9 copy.7
  1.5 0.7 reshape.7.mpo_h
  2.2 126.1 %shard_map.68 = (bf16[128,8,512]{2,1,0:T(8,128)(2,1)}, bf16[128,4,4,512]{3,2,1,0:T(4,128)(2,1)}) custom-call(bf16[128,8,512]{2,1,0:T(8,128)(2,1)} %bitcast.10, bf16[128,4,512]{2,1,0:T(4,128)(2,1)} %bitcast.12, bf16[128,4,4,512]{3,2,1,0:T(4,128)(2,1)} %bitcast.8, bf16[8,512,512]{2,1,0:T(8,128)(2,1)} %bitcast.7, bf16[32,32]{1,0:T(8,128)(2,1)} %reshape.7.mpo_h), custom_call_target="tpu_custom_call" | custom-call | tf_op jit(solution)/shard_map/pallas_call | solution.py:507
  128.3 0.0 copy-start
  128.3 2.4 %copy.10 = bf16[1,128,8,512]{3,2,1,0:T(8,128)(2,1)} copy(bf16[1,128,8,512]{3,2,1,0:T(8,128)(2,1)} %bitcast.11) | data formatting | bytes 2097152
  130.7 0.0 copy-done
  130.7 1.3 copy.11
Async XLA Ops:
  128.3 2.4 %copy-start = (bf16[128,4,4,512]{3,2,1,0:T(4,128)(2,1)S(1)}, bf16[128,4,4,512]{3,2,1,0:T(4,128)(2,1)}, u32[]{:S(2)}) copy-start(bf16[128,4,4,512]{3,2,1,0:T(4,128)(2,1)} %get-tuple-element.5) | copy-start | bytes 6291460

commit v3 on v2

--- a/solution.py
+++ b/solution.py
@@ -185,13 +185,15 @@
                 i = slot((key, q))
                 remote(i, i, region(q, mine), region(q, mine), target).start()
         if last:
+            spread_reg(q)
+
+    def spread_reg(q):
+        if True:
             for key, target in (("psi_y", to_y), ("psi_c", to_c)):
                 i = slot((key, q))
                 started[(key, q)] = [(remote(i, i, region(q, mine), region(q, mine), target), None)]
                 lands[(key, q)] = region(q, mine)
 
-    stays_up = jnp.logical_and(x == 1, core == 1)
-
     def relay(q):
         arrive(("psi_y", q), region(q, across))
         send(("psi_yc", q), region(q, across), region(q, across), to_c)
@@ -200,8 +202,6 @@
         arrive(("psi_c", q), region(q, mates))
         arrive(("psi_yc", q), region(q, corner))
 
-    spread_if(0, psi_self, False)
-    spread_if(1, psi_self, False)
 
     @pl.when(moves)
     def _():
@@ -251,7 +251,7 @@
         arrive(("site_y", p), site.at[pieces[p], block(across), :])
         send(("site_yc", p), site.at[pieces[p], block(across), :], site.at[pieces[p], block(across), :], to_c)
 
-    spread_if(0, stays_up, False)
+    spread_if(0, stays, False)
     for p in range(phys):
         arrive(("site_c", p), site.at[pieces[p], block(mates), :])
         arrive(("site_yc", p), site.at[pieces[p], block(corner), :])
@@ -264,7 +264,7 @@
     for i in range(n_left):
         arrive(("left", i), left.at[left_part(i)])
 
-        @pl.loop(i * per_left, (i + 1) * per_left)
+        @pl.loop(i * per_left, (i + 1) * per_left, unroll=per_left)
         def _(g):
             ours = left[pl.ds(pl.multiple_of(g * group, group), group)].astype(F32)
             ours = ours.reshape(strip, chi).astype(BF16)
@@ -277,7 +277,7 @@
                     second[n, pl.ds(where, group), :] = out[at:at + group, :]
 
         if i == 0:
-            spread_if(1, stays_up, False)
+            spread_if(1, stays, False)
         if i == n_left - 2:
             for q in range(cuts):
                 launch_late(q)
@@ -315,10 +315,10 @@
             total = part[n, rows_of(stage, 1, core), :].astype(F32) + rs1[stage, 1, n].astype(F32)
             send2[stage, n] = total.astype(BF16)
 
-    def send_far(stage):
+    def send_far(stage, when=None):
         for j in range(n_rs):
             where = pl.ds(j * rs_rows, rs_rows)
-            send(("rs2", stage, j), send2.at[stage, :, where, :], rs2.at[stage, :, where, :], to_y)
+            send(("rs2", stage, j), send2.at[stage, :, where, :], rs2.at[stage, :, where, :], to_y, when=when)
 
     def finish(stage):
         arrive(("rs1", stage, 0), rs1.at[stage, 0])
@@ -401,7 +401,6 @@
     add_far(0)
     swap_halves(1)
     send_far(0)
-    spread_if(2, stays, False)
     spread_if(0, moves, True)
 
     side = width * pq
@@ -424,71 +423,93 @@
     spread_if(1, moves, True)
     finish(0)
     home_left(0)
-    spread_if(2, moves, True)
-    spread_if(3, stays, False)
+    spread_if(2, moves, False)
     relay(0)
     arrive(("right",), right)
+    for i in range(cuts):
+        acc[i, batch * pq:2 * batch * pq, :] = jnp.zeros((batch * pq, lanes), F32)
+
+    def contract(stage, q):
+        ours = nl_in[stage]
+        for t in range(pq // 2):
+            mixed[t] = mm(ours, psi[q, t])
+
+    def project(p):
+        here = mixed[:, p * 2 * width:(p + 1) * 2 * width, :]
+        tiles = []
+        for i in range(2):
+            one = here[:, i * width:(i + 1) * width, :].reshape(pq // 2 * width, 2 * lanes)
+            tiles.append(jnp.concatenate([one[:, :lanes], one[:, lanes:]], axis=0))
+        both = jnp.concatenate(tiles, axis=1).astype(BF16)
+        out = mm(pair[...], both).astype(BF16)
+        for i in range(2):
+            where = pl.ds((p * 2 + i) * pq, pq)
+            for k in range(width):
+                proj[where, k * lanes:(k + 1) * lanes] = out[k * pq:(k + 1) * pq, i * lanes:(i + 1) * lanes]
+
+    def environment(q):
+        start = q * lanes if isinstance(q, int) else pl.multiple_of(q * lanes, lanes)
+        return right[:, pl.ds(start, lanes), :].reshape(width * lanes, chi)
+
+    def gathered(where):
+        return jnp.concatenate([acc[i, where, :] for i in range(cuts)], axis=1)
 
     def strip_of(stage, q):
-        ours = nl_in[stage]
-
-        @pl.loop(0, pq // 2)
-        def _(t):
-            mixed[t] = mm(ours, psi[q, t])
-
-        @pl.loop(0, batch // 2, unroll=4)
-        def _(p):
-            here = mixed[:, pl.ds(pl.multiple_of(p * 2 * width, 2 * width), 2 * width), :]
-            tiles = []
-            for i in range(2):
-                one = here[:, i * width:(i + 1) * width, :].reshape(pq // 2 * width, 2 * lanes)
-                tiles.append(jnp.concatenate([one[:, :lanes], one[:, lanes:]], axis=0))
-            both = jnp.concatenate(tiles, axis=1).astype(BF16)
-            out = mm(pair[...], both).astype(BF16)
-            for i in range(2):
-                where = pl.ds(pl.multiple_of((p * 2 + i) * pq, pq), pq)
-                for k in range(width):
-                    piece = out[k * pq:(k + 1) * pq, i * lanes:(i + 1) * lanes]
-                    proj[where, k * lanes:(k + 1) * lanes] = piece
-
-        env = right[:, q * lanes:(q + 1) * lanes, :].reshape(width * lanes, chi)
+        contract(stage, q)
+        for p in range(batch // 2):
+            project(p)
+        total = mm(proj[...], environment(q))
+        where = pl.ds(stage * batch * pq, batch * pq)
+        if not isinstance(q, int) or q > 0:
+            total += gathered(where)
+        for i in range(cuts):
+            acc[i, where, :] = total[:, i * lanes:(i + 1) * lanes]
+
+    def last_strip(stage):
+        q = cuts - 1
+        contract(stage, q)
         high = out_rows * pq
         for j in range(n_out):
-            total = mm(proj[j * high:(j + 1) * high, :], env)
-            long = pl.ds(stage * batch * pq + j * high, high)
-            if q > 0:
-                total += jnp.concatenate([acc[i, long, :] for i in range(cuts)], axis=1)
-            if q < cuts - 1:
-                for i in range(cuts):
-                    acc[i, long, :] = total[:, i * lanes:(i + 1) * lanes]
-            else:
-                out = total.reshape(out_rows, phys, phys, chi).astype(BF16)
-                prod[stage, j * out_rows:(j + 1) * out_rows] = out
-                home_product(stage, j)
+            for p in range(out_rows // 2):
+                project(j * (out_rows // 2) + p)
+            total = mm(proj[j * high:(j + 1) * high, :], environment(q))
+            total += gathered(pl.ds(stage * batch * pq + j * high, high))
+            out = total.reshape(out_rows, phys, phys, chi).astype(BF16)
+            prod[stage, j * out_rows:(j + 1) * out_rows] = out
+            home_product(stage, j)
 
     complete(0)
+    spread_if(2, stays, False)
+    spread_if(3, moves, False)
     for j in range(n_rs):
         high = pl.ds(j * rs_rows * width, rs_rows * width)
         arrive(("up", 0, j), nl_in.at[0, high, :])
     strip_of(0, 0)
     relay(1)
-    spread_if(3, moves, True)
     complete(1)
+    spread_if(3, stays, False)
+    spread_reg(2)
+    spread_reg(3)
     strip_of(0, 1)
     relay(2)
     complete(2)
     strip_of(0, 2)
-    send_far(1)
+    send_far(1, moves)
     relay(3)
     complete(3)
-    strip_of(0, 3)
+    send_far(1, stays)
+    last_strip(0)
     finish(1)
     home_left(1)
     for j in range(n_rs):
         high = pl.ds(j * rs_rows * width, rs_rows * width)
         arrive(("up", 1, j), nl_in.at[1, high, :])
-    for q in range(cuts):
+
+    @pl.loop(0, cuts - 1)
+    def _(q):
         strip_of(1, q)
+
+    last_strip(1)
 
     finalize()
 

time: 132 us -> 116 us (0.88)
  Pallas kernels: 126 us -> 110 us
    pallas_call x1, Pallas kernels: 126 us -> 110 us  [fused(): pl.pallas_call(functools.partial(kernel, (rows, width, phys, chi, group,...]
where the time goes in v3:
time: 116 us
  Pallas kernels  110 us (95%)
  local copies, waits for them, and re-layouts  5.3 us (5%)
    pallas_call x1, Pallas kernels, fused(): pl.pallas_call(functools.partial(kernel, (rows, width, phys, chi, group,...  110 us
    unnamed x4, local copies, waits for them, and re-layouts  3.73 us

profile of v3, /device:TPU:11, one launch (start us, length us, event | category | flops | bytes accessed | tf_op | source)
XLA Modules:
  0.0 116.1 jit_solution(9918007070825238988)
XLA Ops:
  0.6 0.9 copy.7
  1.5 0.7 reshape.7.mpo_h
  2.2 110.1 %shard_map.68 = (bf16[128,8,512]{2,1,0:T(8,128)(2,1)}, bf16[128,4,4,512]{3,2,1,0:T(4,128)(2,1)}) custom-call(bf16[128,8,512]{2,1,0:T(8,128)(2,1)} %bitcast.10, bf16[128,4,512]{2,1,0:T(4,128)(2,1)} %bitcast.12, bf16[128,4,4,512]{3,2,1,0:T(4,128)(2,1)} %bitcast.8, bf16[8,512,512]{2,1,0:T(8,128)(2,1)} %bitcast.7, bf16[32,32]{1,0:T(8,128)(2,1)} %reshape.7.mpo_h), custom_call_target="tpu_custom_call" | custom-call | tf_op jit(solution)/shard_map/pallas_call | solution.py:528
  112.3 0.0 copy-start
  112.4 2.4 %copy.10 = bf16[1,128,8,512]{3,2,1,0:T(8,128)(2,1)} copy(bf16[1,128,8,512]{3,2,1,0:T(8,128)(2,1)} %bitcast.11) | data formatting | bytes 2097152
  114.8 0.0 copy-done
  114.8 1.3 %copy.11 = bf16[1,128,4,4,512]{4,3,2,1,0:T(4,128)(2,1)} copy(bf16[1,128,4,4,512]{4,3,2,1,0:T(4,128)(2,1)S(1)} %bitcast.9) | data formatting | bytes 4194304
Async XLA Ops:
  112.3 2.4 %copy-start = (bf16[128,4,4,512]{3,2,1,0:T(4,128)(2,1)S(1)}, bf16[128,4,4,512]{3,2,1,0:T(4,128)(2,1)}, u32[]{:S(2)}) copy-start(bf16[128,4,4,512]{3,2,1,0:T(4,128)(2,1)} %get-tuple-element.5) | copy-start | bytes 6291460

commit v4 on v3

--- a/solution.py
+++ b/solution.py
@@ -20,7 +20,7 @@
     dims,
     left_h, site_h, psi_h, right_h, mpo_h,
     new_left, product,
-    left, site_raw, psi_raw, mpo, right,
+    left, site_raw, psi_raw, mpo_raw, mpo_f, mpo, right,
     site_own, psi_own, site, site_tr, mix, pair,
     second, part, rs1, send2, rs2, nl_own, nl_out, nl_in, psi, mixed, proj, prod, acc,
     local_sem, send_sem, recv_sem,
@@ -57,7 +57,7 @@
     for i, (name, src, dst) in enumerate((
         ("site", site_h, site_raw),
         ("psi", psi_h, psi_raw),
-        ("mpo", mpo_h, mpo),
+        ("mpo", mpo_h, mpo_raw),
     )):
         loads[name] = pltpu.make_async_copy(src, dst, local_sem.at[i])
         loads[name].start()
@@ -69,7 +69,16 @@
         greeted.append({"sec": lax.rem(mate_sec + dz, n_sec), "bond": side_bond})
     for target in greeted:
         pl.semaphore_signal(barrier, inc=1, device_id=target, device_id_type=MESH)
-    pl.semaphore_wait(barrier, len(greeted))
+
+    lanes = chi // cuts
+    loads["site"].wait()
+    flat = site_raw[...].astype(F32).reshape(rows * phys, chi)
+    for i in range(cuts):
+        acc[i, :rows * phys, :] = flat[:, i * lanes:(i + 1) * lanes]
+    for t in range(phys):
+        for i in range(cuts):
+            tile = acc[i, pl.ds(t, rows, stride=phys), :]
+            site_own[t, :, i * lanes:(i + 1) * lanes] = tile.astype(BF16)
 
     started = {}
     counter = {}
@@ -104,7 +113,6 @@
         landed.add(key)
         remote(i, i, dst, dst, to_c).wait_recv()
 
-    lanes = chi // cuts
     pieces = tuple(pl.ds(t, 1) for t in range(phys))
     n_left = 4
     tall_left = rows // n_left
@@ -116,14 +124,7 @@
         send(("left", i), left_h.at[left_part(i)], left.at[left_part(i)], to_xc, when=moves)
         keep(("left", i), left_h.at[left_part(i)], left.at[left_part(i)], stays)
 
-    loads["site"].wait()
-    flat = site_raw[...].astype(F32).reshape(rows * phys, chi)
-    for i in range(cuts):
-        acc[i, :rows * phys, :] = flat[:, i * lanes:(i + 1) * lanes]
-    for t in range(phys):
-        for i in range(cuts):
-            tile = acc[i, pl.ds(t, rows, stride=phys), :]
-            site_own[t, :, i * lanes:(i + 1) * lanes] = tile.astype(BF16)
+    pl.semaphore_wait(barrier, len(greeted))
 
     def site_spread(p, from_own):
         src = site_own.at[pieces[p]] if from_own else site.at[pieces[p], block(mine), :]
@@ -187,6 +188,8 @@
         if last:
             spread_reg(q)
 
+    stays_up = jnp.logical_and(x == 1, core == 1)
+
     def spread_reg(q):
         if True:
             for key, target in (("psi_y", to_y), ("psi_c", to_c)):
@@ -231,6 +234,15 @@
         return jnp.where(condition, 1.0, 0.0).astype(BF16)
 
     small = phys * width
+    codes = width * width
+    pick_n = one_hot(lax.rem(iota((width, codes), 1), width) == iota((width, codes), 0))
+    same_m = lax.div(iota((codes, small), 0), width) == lax.rem(iota((codes, small), 1), width)
+    for u in range(phys):
+        col_s = lax.div(iota((pq, small), 1), width)
+        spread_s = one_hot(iota((pq, small), 0) == col_s * phys + u)
+        chosen = jnp.where(same_m, mm(mpo_raw[...], spread_s), 0.0).astype(BF16)
+        mpo_f[u * width:(u + 1) * width, :] = mm(pick_n, chosen)
+    mpo[...] = mpo_f[...].astype(BF16)
     big = small * group
     tall_code = lax.div(iota((big, small), 0), group)
     spread_rows = one_hot(tall_code == iota((big, small), 1))
@@ -247,11 +259,12 @@
             tile = own[:, i * lanes:(i + 1) * lanes]
             site_tr[i * lanes:(i + 1) * lanes, t * rows:(t + 1) * rows] = tile.T.astype(BF16)
 
+    spread_if(0, stays, False)
     for p in range(phys):
         arrive(("site_y", p), site.at[pieces[p], block(across), :])
         send(("site_yc", p), site.at[pieces[p], block(across), :], site.at[pieces[p], block(across), :], to_c)
 
-    spread_if(0, stays, False)
+    spread_if(1, psi_self, False)
     for p in range(phys):
         arrive(("site_c", p), site.at[pieces[p], block(mates), :])
         arrive(("site_yc", p), site.at[pieces[p], block(corner), :])
@@ -277,10 +290,11 @@
                     second[n, pl.ds(where, group), :] = out[at:at + group, :]
 
         if i == 0:
-            spread_if(1, stays, False)
+            spread_if(1, stays_up, False)
         if i == n_left - 2:
             for q in range(cuts):
                 launch_late(q)
+            spread_if(2, stays, False)
 
 
     hrows = rows // 2
@@ -320,10 +334,11 @@
             where = pl.ds(j * rs_rows, rs_rows)
             send(("rs2", stage, j), send2.at[stage, :, where, :], rs2.at[stage, :, where, :], to_y, when=when)
 
-    def finish(stage):
-        arrive(("rs1", stage, 0), rs1.at[stage, 0])
+    def finish(stage, parts):
+        if parts[0] == 0:
+            arrive(("rs1", stage, 0), rs1.at[stage, 0])
         base = stage * hrows * width
-        for j in range(n_rs):
+        for j in parts:
             where = pl.ds(j * rs_rows, rs_rows)
             arrive(("rs2", stage, j), rs2.at[stage, :, where, :])
             yy = y
@@ -421,7 +436,7 @@
 
     add_far(1)
     spread_if(1, moves, True)
-    finish(0)
+    finish(0, range(n_rs))
     home_left(0)
     spread_if(2, moves, False)
     relay(0)
@@ -429,10 +444,10 @@
     for i in range(cuts):
         acc[i, batch * pq:2 * batch * pq, :] = jnp.zeros((batch * pq, lanes), F32)
 
-    def contract(stage, q):
-        ours = nl_in[stage]
+    def contract(stage, q, lo, n):
+        ours = nl_in[stage, lo * width:(lo + n) * width, :]
         for t in range(pq // 2):
-            mixed[t] = mm(ours, psi[q, t])
+            mixed[t, :n * width, :] = mm(ours, psi[q, t])
 
     def project(p):
         here = mixed[:, p * 2 * width:(p + 1) * 2 * width, :]
@@ -454,32 +469,33 @@
     def gathered(where):
         return jnp.concatenate([acc[i, where, :] for i in range(cuts)], axis=1)
 
-    def strip_of(stage, q):
-        contract(stage, q)
-        for p in range(batch // 2):
+    def strip_of(stage, q, lo=0, n=None):
+        n = batch if n is None else n
+        contract(stage, q, lo, n)
+        for p in range(n // 2):
             project(p)
-        total = mm(proj[...], environment(q))
-        where = pl.ds(stage * batch * pq, batch * pq)
+        total = mm(proj[:n * pq, :], environment(q))
+        where = pl.ds((stage * batch + lo) * pq, n * pq)
         if not isinstance(q, int) or q > 0:
             total += gathered(where)
         for i in range(cuts):
             acc[i, where, :] = total[:, i * lanes:(i + 1) * lanes]
 
-    def last_strip(stage):
+    def last_strip(stage, lo=0, n=None):
+        n = batch if n is None else n
         q = cuts - 1
-        contract(stage, q)
+        contract(stage, q, lo, n)
         high = out_rows * pq
-        for j in range(n_out):
+        for j in range(n // out_rows):
             for p in range(out_rows // 2):
                 project(j * (out_rows // 2) + p)
             total = mm(proj[j * high:(j + 1) * high, :], environment(q))
-            total += gathered(pl.ds(stage * batch * pq + j * high, high))
+            total += gathered(pl.ds((stage * batch + lo) * pq + j * high, high))
             out = total.reshape(out_rows, phys, phys, chi).astype(BF16)
-            prod[stage, j * out_rows:(j + 1) * out_rows] = out
-            home_product(stage, j)
+            prod[stage, lo + j * out_rows:lo + (j + 1) * out_rows] = out
+            home_product(stage, lo // out_rows + j)
 
     complete(0)
-    spread_if(2, stays, False)
     spread_if(3, moves, False)
     for j in range(n_rs):
         high = pl.ds(j * rs_rows * width, rs_rows * width)
@@ -499,18 +515,32 @@
     complete(3)
     send_far(1, stays)
     last_strip(0)
-    finish(1)
+    def landed_rows(stage, parts):
+        for j in parts:
+            high = pl.ds(j * rs_rows * width, rs_rows * width)
+            arrive(("up", stage, j), nl_in.at[stage, high, :])
+
+    few = batch // 2
+    early_parts, late_parts = range(n_rs // 2), range(n_rs // 2, n_rs)
+    finish(1, early_parts)
+    landed_rows(1, early_parts)
+
+    @pl.loop(0, cuts // 2)
+    def _(q):
+        strip_of(1, q, 0, few)
+
+    finish(1, late_parts)
     home_left(1)
-    for j in range(n_rs):
-        high = pl.ds(j * rs_rows * width, rs_rows * width)
-        arrive(("up", 1, j), nl_in.at[1, high, :])
+    for q in range(cuts // 2, cuts - 1):
+        strip_of(1, q, 0, few)
+    last_strip(1, 0, few)
+    landed_rows(1, late_parts)
 
     @pl.loop(0, cuts - 1)
     def _(q):
-        strip_of(1, q)
-
-    last_strip(1)
-
+        strip_of(1, q, few, few)
+
+    last_strip(1, few, few)
     finalize()
 
 
@@ -521,10 +551,9 @@
     group, cuts, batch = 16, 4, rows // 2
     lanes = chi // cuts
     small = phys * width
-    table = mpo.transpose(3, 1, 2, 0).reshape(small, small)
+    table = mpo.reshape(width * width, pq)
     n_sems = 120
     any_spec = pl.BlockSpec(memory_space=pl.ANY)
-    vmem = pl.BlockSpec(memory_space=pltpu.VMEM)
     new_left, product = pl.pallas_call(
         functools.partial(kernel, (rows, width, phys, chi, group, cuts, batch)),
         out_shape=(
@@ -532,11 +561,13 @@
             jax.ShapeDtypeStruct((rows, phys, phys, chi), BF16),
         ),
         in_specs=[any_spec] * 5,
-        out_specs=(vmem, vmem),
+        out_specs=(any_spec, any_spec),
         scratch_shapes=[
             pltpu.VMEM((rows, width, chi), BF16),
             pltpu.VMEM((rows, phys, chi), BF16),
             pltpu.VMEM((rows, phys, phys, chi), BF16),
+            pltpu.VMEM((width * width, pq), BF16),
+            pltpu.VMEM((small, small), F32),
             pltpu.VMEM((small, small), BF16),
             pltpu.VMEM((width, chi, chi), BF16),
             pltpu.VMEM((phys, rows, chi), BF16),

time: 116 us -> 113 us (0.974); the launches traced: 116 us -> 111 us
  Pallas kernels: 110 us -> 105 us
    pallas_call x1, Pallas kernels: 110 us -> 105 us  [fused(): pl.pallas_call(functools.partial(kernel, (rows, width, phys, chi, group,...]
    unnamed x4 -> x5, local copies, waits for them, and re-layouts: 3.73 us -> 4.5 us
where the time goes in v4:
time: 113 us; the launch traced here: 111 us
  Pallas kernels  105 us (93%)
  local copies, waits for them, and re-layouts  5.3 us (5%)
    pallas_call x1, Pallas kernels, fused(): pl.pallas_call(functools.partial(kernel, (rows, width, phys, chi, group,...  105 us
    unnamed x5, local copies, waits for them, and re-layouts  4.5 us

profile of v4, /device:TPU:11, one launch (start us, length us, event | category | flops | bytes accessed | tf_op | source)
XLA Modules:
  0.0 110.8 jit_solution(12953613436128628322)
XLA Ops:
  0.6 0.8 copy.8
  1.4 0.1 reshape.7
  1.5 0.7 copy.9.mpo_h
  2.2 104.8 %shard_map.68 = (bf16[128,8,512]{2,1,0:T(8,128)(2,1)}, bf16[128,4,4,512]{3,2,1,0:T(4,128)(2,1)}) custom-call(bf16[128,8,512]{2,1,0:T(8,128)(2,1)} %bitcast.13, bf16[128,4,512]{2,1,0:T(4,128)(2,1)} %bitcast.15, bf16[128,4,4,512]{3,2,1,0:T(4,128)(2,1)} %bitcast.12, bf16[8,512,512]{2,1,0:T(8,128)(2,1)} %bitcast.10, bf16[64,16]{1,0:T(8,128)(2,1)} %copy.9.mpo_h), custom_call_target="tpu_custom_call" | custom-call | tf_op jit(solution)/shard_map/pallas_call | solution.py:557
  107.0 0.0 copy-start
  107.0 2.4 %copy.12 = bf16[1,128,8,512]{3,2,1,0:T(8,128)(2,1)} copy(bf16[1,128,8,512]{3,2,1,0:T(8,128)(2,1)} %bitcast.14) | data formatting | bytes 2097152
  109.4 0.0 copy-done
  109.4 1.3 %copy.13 = bf16[1,128,4,4,512]{4,3,2,1,0:T(4,128)(2,1)} copy(bf16[1,128,4,4,512]{4,3,2,1,0:T(4,128)(2,1)S(1)} %bitcast.11) | data formatting | bytes 4194304
Async XLA Ops:
  107.0 2.4 %copy-start = (bf16[128,4,4,512]{3,2,1,0:T(4,128)(2,1)S(1)}, bf16[128,4,4,512]{3,2,1,0:T(4,128)(2,1)}, u32[]{:S(2)}) copy-start(bf16[128,4,4,512]{3,2,1,0:T(4,128)(2,1)} %get-tuple-element.5) | copy-start | bytes 6291460

commit v5 on v4

--- a/solution.py
+++ b/solution.py
@@ -20,10 +20,10 @@
     dims,
     left_h, site_h, psi_h, right_h, mpo_h,
     new_left, product,
-    left, site_raw, psi_raw, mpo_raw, mpo_f, mpo, right,
+    left, site_raw, psi_raw, mpo_raw, mpo, right,
     site_own, psi_own, site, site_tr, mix, pair,
     second, part, rs1, send2, rs2, nl_own, nl_out, nl_in, psi, mixed, proj, prod, acc,
-    local_sem, send_sem, recv_sem,
+    local_sem, send_sem, recv_sem, chain,
 ):
     rows, width, phys, chi, group, cuts, batch = dims
     pq = phys * phys
@@ -64,11 +64,19 @@
 
     barrier = pltpu.get_barrier_semaphore()
     greeted = [to_c, to_y, to_x, to_xc]
-    for dz in (2, n_sec - 2):
-        greeted.append({"sec": lax.rem(sec + dz, n_sec)})
-        greeted.append({"sec": lax.rem(mate_sec + dz, n_sec), "bond": side_bond})
     for target in greeted:
         pl.semaphore_signal(barrier, inc=1, device_id=target, device_id_type=MESH)
+    top = n_sec // 2 - 1
+    down = lax.rem(sec + n_sec - 2, n_sec)
+    down_xc = {"sec": lax.rem(mate_sec + n_sec - 2, n_sec), "bond": side_bond}
+
+    def tell(semaphore, target):
+        pl.semaphore_signal(semaphore, inc=1, device_id=target, device_id_type=MESH)
+
+    pl.when(jnp.logical_and(x == 1, z > 0))(lambda: tell(barrier, {"sec": down}))
+    pl.when(jnp.logical_and(jnp.logical_and(x == 1, core == 0), z > 0))(lambda: tell(barrier, down_xc))
+    climbs = jnp.logical_or(x == 1, core == 1)
+    below_top = jnp.logical_and(climbs, z < top)
 
     lanes = chi // cuts
     loads["site"].wait()
@@ -124,7 +132,8 @@
         send(("left", i), left_h.at[left_part(i)], left.at[left_part(i)], to_xc, when=moves)
         keep(("left", i), left_h.at[left_part(i)], left.at[left_part(i)], stays)
 
-    pl.semaphore_wait(barrier, len(greeted))
+    pl.semaphore_wait(barrier, len(greeted) + jnp.where(below_top, 1, 0))
+    pl.when(jnp.logical_and(x == 1, z == 0))(lambda: tell(chain.at[0], {"sec": up}))
 
     def site_spread(p, from_own):
         src = site_own.at[pieces[p]] if from_own else site.at[pieces[p], block(mine), :]
@@ -138,6 +147,12 @@
         site_spread(p, True)
     for i in range(n_left):
         send_left(i)
+
+
+    @pl.when(jnp.logical_and(x == 1, jnp.logical_and(z > 0, z < top)))
+    def _():
+        pl.semaphore_wait(chain.at[0], 1)
+        tell(chain.at[0], {"sec": up})
 
     loads["psi"].wait()
     tall = 8
@@ -174,9 +189,14 @@
             at = (t % 2) * lanes
             tile = acc[q, pl.ds(t, rows, stride=pq), :]
             psi_own[q, t // 2, :, at:at + lanes] = tile.astype(BF16)
-        if q > 0:
-            launch(q - 1)
-    launch(cuts - 1)
+
+    @pl.when(jnp.logical_and(x == 1, z == top))
+    def _():
+        pl.semaphore_wait(chain.at[0], 1)
+        pl.when(core == 0)(lambda: tell(chain.at[1], to_xc))
+
+    for q in range(cuts):
+        launch(q)
 
     def spread_if(q, when, last):
         @pl.when(when)
@@ -234,15 +254,16 @@
         return jnp.where(condition, 1.0, 0.0).astype(BF16)
 
     small = phys * width
-    codes = width * width
-    pick_n = one_hot(lax.rem(iota((width, codes), 1), width) == iota((width, codes), 0))
-    same_m = lax.div(iota((codes, small), 0), width) == lax.rem(iota((codes, small), 1), width)
-    for u in range(phys):
-        col_s = lax.div(iota((pq, small), 1), width)
-        spread_s = one_hot(iota((pq, small), 0) == col_s * phys + u)
-        chosen = jnp.where(same_m, mm(mpo_raw[...], spread_s), 0.0).astype(BF16)
-        mpo_f[u * width:(u + 1) * width, :] = mm(pick_n, chosen)
-    mpo[...] = mpo_f[...].astype(BF16)
+    codes = width * pq
+    flat = mpo_raw[...].astype(F32).reshape(codes, width).astype(BF16)
+    spread_n = one_hot(lax.rem(iota((width, small), 1), width) == iota((width, small), 0))
+    same_u = lax.rem(iota((codes, small), 0), phys) == lax.div(iota((codes, small), 1), width)
+    tall_un = jnp.where(same_u, mm(flat, spread_n), 0.0).astype(BF16)
+    code = iota((codes, small), 0)
+    code_sm = lax.rem(lax.div(code, phys), phys) * width + lax.div(code, pq)
+    pick_sm = one_hot(code_sm == iota((codes, small), 1))
+    over_codes = (((0,), (0,)), ((), ()))
+    mpo[...] = lax.dot_general(tall_un, pick_sm, over_codes, preferred_element_type=F32).astype(BF16)
     big = small * group
     tall_code = lax.div(iota((big, small), 0), group)
     spread_rows = one_hot(tall_code == iota((big, small), 1))
@@ -292,6 +313,7 @@
         if i == 0:
             spread_if(1, stays_up, False)
         if i == n_left - 2:
+            pl.when(jnp.logical_and(psi_waits, z == top))(lambda: pl.semaphore_wait(chain.at[1], 1))
             for q in range(cuts):
                 launch_late(q)
             spread_if(2, stays, False)
@@ -525,14 +547,14 @@
     finish(1, early_parts)
     landed_rows(1, early_parts)
 
-    @pl.loop(0, cuts // 2)
+    strip_of(1, 0, 0, few)
+
+    finish(1, late_parts)
+    home_left(1)
+    @pl.loop(1, cuts - 1)
     def _(q):
         strip_of(1, q, 0, few)
 
-    finish(1, late_parts)
-    home_left(1)
-    for q in range(cuts // 2, cuts - 1):
-        strip_of(1, q, 0, few)
     last_strip(1, 0, few)
     landed_rows(1, late_parts)
 
@@ -551,7 +573,7 @@
     group, cuts, batch = 16, 4, rows // 2
     lanes = chi // cuts
     small = phys * width
-    table = mpo.reshape(width * width, pq)
+    table = mpo.transpose(0, 2, 3, 1)
     n_sems = 120
     any_spec = pl.BlockSpec(memory_space=pl.ANY)
     new_left, product = pl.pallas_call(
@@ -566,8 +588,7 @@
             pltpu.VMEM((rows, width, chi), BF16),
             pltpu.VMEM((rows, phys, chi), BF16),
             pltpu.VMEM((rows, phys, phys, chi), BF16),
-            pltpu.VMEM((width * width, pq), BF16),
-            pltpu.VMEM((small, small), F32),
+            pltpu.VMEM((width, phys, phys, width), BF16),
             pltpu.VMEM((small, small), BF16),
             pltpu.VMEM((width, chi, chi), BF16),
             pltpu.VMEM((phys, rows, chi), BF16),
@@ -592,6 +613,7 @@
             pltpu.SemaphoreType.DMA((6,)),
             pltpu.SemaphoreType.DMA((n_sems,)),
             pltpu.SemaphoreType.DMA((n_sems,)),
+            pltpu.SemaphoreType.REGULAR((2,)),
         ],
         compiler_params=pltpu.CompilerParams(
             collective_id=0, has_side_effects=True, vmem_limit_bytes=62 * 1024 * 1024

time: 113 us -> 108 us (0.956); the launches traced: 111 us -> 107 us
  Pallas kernels: 105 us -> 103 us
  local copies, waits for them, and re-layouts: 5.3 us -> 3.73 us
    pallas_call x1, Pallas kernels: 105 us -> 103 us  [fused(): pl.pallas_call(functools.partial(kernel, (rows, width, phys, chi, group,...]
    unnamed x5 -> x4, local copies, waits for them, and re-layouts: 4.5 us -> 3.73 us
where the time goes in v5:
time: 108 us; the launch traced here: 107 us
  Pallas kernels  103 us (95%)
  local copies, waits for them, and re-layouts  3.73 us (3%)
    pallas_call x1, Pallas kernels, fused(): pl.pallas_call(functools.partial(kernel, (rows, width, phys, chi, group,...  103 us
    unnamed x4, local copies, waits for them, and re-layouts  3.73 us

profile of v5, /device:TPU:11, one launch (start us, length us, event | category | flops | bytes accessed | tf_op | source)
XLA Modules:
  0.0 107.2 jit_solution(11355725057637689334)
XLA Ops:
  0.6 102.8 %shard_map.68 = (bf16[128,8,512]{2,1,0:T(8,128)(2,1)}, bf16[128,4,4,512]{3,2,1,0:T(4,128)(2,1)}) custom-call(bf16[128,8,512]{2,1,0:T(8,128)(2,1)} %bitcast.10, bf16[128,4,512]{2,1,0:T(4,128)(2,1)} %bitcast.12, bf16[128,4,4,512]{3,2,1,0:T(4,128)(2,1)} %bitcast.9, bf16[8,512,512]{2,1,0:T(8,128)(2,1)} %bitcast.7, bf16[8,4,4,8]{3,2,1,0:T(4,128)(2,1)} %bitcast.13), custom_call_target="tpu_custom_call" | custom-call | tf_op jit(solution)/shard_map/pallas_call | solution.py:579
  103.4 0.0 copy-start
  103.4 2.4 %copy.9 = bf16[1,128,8,512]{3,2,1,0:T(8,128)(2,1)} copy(bf16[1,128,8,512]{3,2,1,0:T(8,128)(2,1)} %bitcast.11) | data formatting | bytes 2097152
  105.9 0.0 copy-done
  105.9 1.3 %copy.10 = bf16[1,128,4,4,512]{4,3,2,1,0:T(4,128)(2,1)} copy(bf16[1,128,4,4,512]{4,3,2,1,0:T(4,128)(2,1)S(1)} %bitcast.8) | data formatting | bytes 4194304
Async XLA Ops:
  103.4 2.4 %copy-start = (bf16[128,4,4,512]{3,2,1,0:T(4,128)(2,1)S(1)}, bf16[128,4,4,512]{3,2,1,0:T(4,128)(2,1)}, u32[]{:S(2)}) copy-start(bf16[128,4,4,512]{3,2,1,0:T(4,128)(2,1)} %get-tuple-element.5) | copy-start | bytes 6291460

commit v6 on v5

--- a/solution.py
+++ b/solution.py
@@ -619,7 +619,40 @@
             collective_id=0, has_side_effects=True, vmem_limit_bytes=62 * 1024 * 1024
         ),
     )(left_env[0], site[0], psi[0], right_env[0], table)
-    return new_left[None], product[None]
+    return settle(new_left, product)
+
+
+def settle(*arrays):
+    cut = 4
+
+    def body(*refs):
+        n = len(arrays)
+        srcs, dsts, tmps, sem = refs[:n], refs[n:2 * n], refs[2 * n:3 * n], refs[3 * n]
+        moves = []
+        for i in reversed(range(n)):
+            step = arrays[i].shape[0] // cut
+            for j in range(cut):
+                part = pl.ds(j * step, step)
+                come = pltpu.make_async_copy(srcs[i].at[part], tmps[i].at[part], sem.at[0, i, j])
+                go = pltpu.make_async_copy(tmps[i].at[part], dsts[i].at[0, part], sem.at[1, i, j])
+                come.start()
+                moves.append((come, go))
+        for come, go in moves:
+            come.wait()
+            go.start()
+        for _, go in moves:
+            go.wait()
+
+    spec = pl.BlockSpec(memory_space=pl.ANY)
+    return pl.pallas_call(
+        body,
+        out_shape=tuple(jax.ShapeDtypeStruct((1,) + a.shape, a.dtype) for a in arrays),
+        in_specs=[spec] * len(arrays),
+        out_specs=(spec,) * len(arrays),
+        scratch_shapes=[pltpu.VMEM(a.shape, a.dtype) for a in arrays]
+        + [pltpu.SemaphoreType.DMA((2, len(arrays), cut))],
+        compiler_params=pltpu.CompilerParams(vmem_limit_bytes=62 * 1024 * 1024),
+    )(*arrays)
 
 
 def shifted(block, axis, distance):

time: 108 us -> 107 us (level)
  local copies, waits for them, and re-layouts: 3.73 us -> 0 us
  Pallas kernels: 103 us -> 106 us
    unnamed x4 -> x0, local copies, waits for them, and re-layouts: 3.73 us -> none
    pallas_call x0 -> x1, Pallas kernels: none -> 2.83 us  [settle(): pl.pallas_call(body, out_shape=tuple((jax.ShapeDtypeStruct((1,) + a.shape...]
where the time goes in v6:
time: 107 us; the launch traced here: 106 us
  Pallas kernels  106 us (99%)
    pallas_call x1, Pallas kernels, fused(): pl.pallas_call(functools.partial(kernel, (rows, width, phys, chi, group,...  103 us
    pallas_call x1, Pallas kernels, settle(): pl.pallas_call(body, out_shape=tuple((jax.ShapeDtypeStruct((1,) + a.shape...  2.83 us

profile of v6, /device:TPU:11, one launch (start us, length us, event | category | flops | bytes accessed | tf_op | source)
XLA Modules:
  0.0 106.5 jit_solution(3947678868691998100)
XLA Ops:
  0.6 102.8 %shard_map.68 = (bf16[128,8,512]{2,1,0:T(8,128)(2,1)}, bf16[128,4,4,512]{3,2,1,0:T(4,128)(2,1)}) custom-call(bf16[128,8,512]{2,1,0:T(8,128)(2,1)} %bitcast.7, bf16[128,4,512]{2,1,0:T(4,128)(2,1)} %bitcast.8, bf16[128,4,4,512]{3,2,1,0:T(4,128)(2,1)} %bitcast.6, bf16[8,512,512]{2,1,0:T(8,128)(2,1)} %bitcast.5, bf16[8,4,4,8]{3,2,1,0:T(4,128)(2,1)} %bitcast.9), custom_call_target="tpu_custom_call" | custom-call | tf_op jit(solution)/shard_map/pallas_call | solution.py:579
  103.4 2.8 %shard_map.69 = (bf16[1,128,8,512]{3,2,1,0:T(8,128)(2,1)}, bf16[1,128,4,4,512]{4,3,2,1,0:T(4,128)(2,1)}) custom-call(bf16[128,8,512]{2,1,0:T(8,128)(2,1)} %get-tuple-element.4.refs_0_, bf16[128,4,4,512]{3,2,1,0:T(4,128)(2,1)} %get-tuple-element.5.refs_1_), custom_call_target="tpu_custom_call" | custom-call | tf_op jit(solution)/shard_map/pallas_call | solution.py:647

commit v7 on v6

--- a/solution.py
+++ b/solution.py
@@ -466,10 +466,10 @@
     for i in range(cuts):
         acc[i, batch * pq:2 * batch * pq, :] = jnp.zeros((batch * pq, lanes), F32)
 
-    def contract(stage, q, lo, n):
+    def contract(stage, q, lo, n, at=0):
         ours = nl_in[stage, lo * width:(lo + n) * width, :]
         for t in range(pq // 2):
-            mixed[t, :n * width, :] = mm(ours, psi[q, t])
+            mixed[t, at * width:(at + n) * width, :] = mm(ours, psi[q, t])
 
     def project(p):
         here = mixed[:, p * 2 * width:(p + 1) * 2 * width, :]
@@ -491,27 +491,27 @@
     def gathered(where):
         return jnp.concatenate([acc[i, where, :] for i in range(cuts)], axis=1)
 
-    def strip_of(stage, q, lo=0, n=None):
+    def strip_of(stage, q, lo=0, n=None, at=0):
         n = batch if n is None else n
-        contract(stage, q, lo, n)
+        contract(stage, q, lo, n, at)
         for p in range(n // 2):
-            project(p)
-        total = mm(proj[:n * pq, :], environment(q))
+            project(at // 2 + p)
+        total = mm(proj[at * pq:(at + n) * pq, :], environment(q))
         where = pl.ds((stage * batch + lo) * pq, n * pq)
         if not isinstance(q, int) or q > 0:
             total += gathered(where)
         for i in range(cuts):
             acc[i, where, :] = total[:, i * lanes:(i + 1) * lanes]
 
-    def last_strip(stage, lo=0, n=None):
+    def last_strip(stage, lo=0, n=None, at=0):
         n = batch if n is None else n
         q = cuts - 1
-        contract(stage, q, lo, n)
+        contract(stage, q, lo, n, at)
         high = out_rows * pq
         for j in range(n // out_rows):
             for p in range(out_rows // 2):
-                project(j * (out_rows // 2) + p)
-            total = mm(proj[j * high:(j + 1) * high, :], environment(q))
+                project(at // 2 + j * (out_rows // 2) + p)
+            total = mm(proj[at * pq + j * high:at * pq + (j + 1) * high, :], environment(q))
             total += gathered(pl.ds((stage * batch + lo) * pq + j * high, high))
             out = total.reshape(out_rows, phys, phys, chi).astype(BF16)
             prod[stage, lo + j * out_rows:lo + (j + 1) * out_rows] = out
@@ -551,18 +551,14 @@
 
     finish(1, late_parts)
     home_left(1)
-    @pl.loop(1, cuts - 1)
-    def _(q):
-        strip_of(1, q, 0, few)
-
-    last_strip(1, 0, few)
+    for q in range(1, cuts - 1):
+        strip_of(1, q, 0, few, q % 2 * few)
+    last_strip(1, 0, few, (cuts - 1) % 2 * few)
     landed_rows(1, late_parts)
 
-    @pl.loop(0, cuts - 1)
-    def _(q):
-        strip_of(1, q, few, few)
-
-    last_strip(1, few, few)
+    for q in range(cuts - 1):
+        strip_of(1, q, few, few, q % 2 * few)
+    last_strip(1, few, few, (cuts - 1) % 2 * few)
     finalize()
 
 

time: 107 us -> 107 us (level)
  no operation moved by 1% of the time
where the time goes in v7:
time: 107 us; the launch traced here: 106 us
  Pallas kernels  105 us (98%)
    pallas_call x1, Pallas kernels, fused(): pl.pallas_call(functools.partial(kernel, (rows, width, phys, chi, group,...  102 us
    pallas_call x1, Pallas kernels, settle(): pl.pallas_call(body, out_shape=tuple((jax.ShapeDtypeStruct((1,) + a.shape...  2.83 us

profile of v7, /device:TPU:11, one launch (start us, length us, event | category | flops | bytes accessed | tf_op | source)
XLA Modules:
  0.0 106.0 jit_solution(4289670596768644735)
XLA Ops:
  0.6 102.3 %shard_map.68 = (bf16[128,8,512]{2,1,0:T(8,128)(2,1)}, bf16[128,4,4,512]{3,2,1,0:T(4,128)(2,1)}) custom-call(bf16[128,8,512]{2,1,0:T(8,128)(2,1)} %bitcast.7, bf16[128,4,512]{2,1,0:T(4,128)(2,1)} %bitcast.8, bf16[128,4,4,512]{3,2,1,0:T(4,128)(2,1)} %bitcast.6, bf16[8,512,512]{2,1,0:T(8,128)(2,1)} %bitcast.5, bf16[8,4,4,8]{3,2,1,0:T(4,128)(2,1)} %bitcast.9), custom_call_target="tpu_custom_call" | custom-call | tf_op jit(solution)/shard_map/pallas_call | solution.py:575
  102.9 2.8 %shard_map.69 = (bf16[1,128,8,512]{3,2,1,0:T(8,128)(2,1)}, bf16[1,128,4,4,512]{4,3,2,1,0:T(4,128)(2,1)}) custom-call(bf16[128,8,512]{2,1,0:T(8,128)(2,1)} %get-tuple-element.4.refs_0_, bf16[128,4,4,512]{3,2,1,0:T(4,128)(2,1)} %get-tuple-element.5.refs_1_), custom_call_target="tpu_custom_call" | custom-call | tf_op jit(solution)/shard_map/pallas_call | solution.py:643
